TPU v7x, 128 devices: a whole 4x4x4 slice. The times are simulated.
128 devices in a mesh: cuts: 32 (over x, y, core), tile: 4 (over z).
Axes of the slice: x: 4, y: 4, z: 4, core: 2. Of those that a mesh axis runs over, the one named last changes fastest.
Arguments:
- probes: float32 [32, 8, 16, 4, 128], P('cuts', None, None, 'tile'), may hold values from -6 to 6
- test_block: float32 [32, 8, 16, 4, 128], P('cuts', None, None, 'tile'), may hold values from -6 to 6
- band_edge: float32 [8, 4, 128], P(None, 'tile'), may hold values from -3 to 3
- slice_hop: float32 [8], replicated, may hold values from 0.5 to 40
- cross_hop: float32 [2, 8, 8], replicated, may hold values from -0.4 to 0.4
- deform: float32 [6, 8, 8], replicated, may hold values from -0.4 to 0.4
- strain_elastic: float32 [32, 16, 6, 32], P('cuts', 'tile'), may hold values from -1 to 1
- strain_ids: int32 [16], replicated, may hold values from 0 to 15, as said below
Outputs:
- moment_fields: float32 [2, 2, 32, 8, 16, 4, 128], P(None, None, 'cuts', None, None, 'tile')
- projected: float32 [4, 2, 16, 16], replicated
Inputs may be any that keep to these rules, and one draw needn't show every extreme that they name: strain_ids is a permutation; subtile g belongs to index g // 4 of tile, and slots i belong to index i // 4. The 4 slots of one index of tile hold at most 2 subtiles belonging to any one index, and exactly 2 for some index.
All inputs are finite; a program needn't handle non-finite values.
Results may differ from a plain program's by a relative error of at most 0.0085.
Values sent between devices are 32-bit elements; how exact they have to be, the bound alone decides.
No kernel may reach another device: no remote copies, remote signals or barrier semaphores. Data moves between devices by JAX's collectives and lax.ppermute only.
A program may use at most 128 MiB of HBM per device.

v0:
```python
import math

import jax
import jax.numpy as jnp
import numpy as np
from jax import lax
from jax.sharding import PartitionSpec as P

PTS = 8
NMOM = 4


HIGHEST = lax.Precision.HIGHEST


def extended(block, sides, width):
    for axis, dim in sides:
        count = lax.axis_size(axis)
        forward = [(i, i + 1) for i in range(count - 1)]
        backward = [(target, source) for source, target in forward]
        low = lax.ppermute(
            lax.slice_in_dim(block, block.shape[dim] - width, None, axis=dim), axis, forward
        )
        high = lax.ppermute(lax.slice_in_dim(block, 0, width, axis=dim), axis, backward)
        block = jnp.concatenate([low, block, high], axis=dim)
    return block


def from_root(array, axis, root):
    mine = lax.axis_index(axis) == root
    return lax.psum(jnp.where(mine, array, jnp.zeros_like(array)), axis)


def prefix_2(array, axis, combine, identity, reverse):
    size, place = (lax.axis_size(axis), lax.axis_index(axis))
    everything = jax.tree.map(lambda part: lax.all_gather(part, axis), array)
    start = jax.tree.map(
        lambda part, zero: jnp.broadcast_to(jnp.asarray(zero, part.dtype), part.shape),
        array,
        identity,
    )

    def hop(k, before):
        at = size - 1 - k if reverse else k
        reached = at > place if reverse else at < place
        new = combine(before, jax.tree.map(lambda part: part[at], everything))
        return jax.tree.map(lambda a, b: jnp.where(reached, a, b), new, before)

    return lax.fori_loop(0, size, hop, start)


def complex_times(former, latter):
    return jnp.stack(
        [
            former[0] * latter[0] - former[1] * latter[1],
            former[0] * latter[1] + former[1] * latter[0],
        ]
    )


def complex_inverse(number):
    square = number[0] * number[0] + number[1] * number[1]
    return jnp.stack([number[0] / square, -number[1] / square])


def complex_power(base_value, exponent, bit_count):
    result = jnp.stack([jnp.ones_like(base_value[0]), jnp.zeros_like(base_value[0])])
    squared = base_value
    for bit_index in range(bit_count):
        bit_set = exponent // 2**bit_index % 2
        result = jnp.where(bit_set == 1, complex_times(result, squared), result)
        squared = complex_times(squared, squared)
    return result


def line_ratio(band_edge, slice_hop, real_part, imag_part):
    hopping = slice_hop[:, None, None]
    ratio_re = (real_part - band_edge) / hopping
    ratio_im = (imag_part + 0.0 * band_edge) / hopping
    disc_re = ratio_re * ratio_re - ratio_im * ratio_im - 4.0
    disc_im = 2.0 * ratio_re * ratio_im
    modulus = jnp.sqrt(disc_re * disc_re + disc_im * disc_im)
    root_re = jnp.sqrt(jnp.maximum(0.5 * (modulus + disc_re), 0.0))
    root_im = jnp.sqrt(jnp.maximum(0.5 * (modulus - disc_re), 0.0)) * jnp.where(
        disc_im >= 0.0, 1.0, -1.0
    )
    lower_re = 0.5 * (ratio_re - root_re)
    lower_im = 0.5 * (ratio_im - root_im)
    upper_re = 0.5 * (ratio_re + root_re)
    upper_im = 0.5 * (ratio_im + root_im)
    choose_low = (
        lower_re * lower_re + lower_im * lower_im <= upper_re * upper_re + upper_im * upper_im
    )
    alpha_re = jnp.where(choose_low, lower_re, upper_re)
    alpha_im = jnp.where(choose_low, lower_im, upper_im)
    return jnp.stack([-alpha_re, -alpha_im])


def relayout_strain(strain_elastic, strain_ids, rows, cols):
    tile_count = lax.axis_size("tile")
    my_tile = lax.axis_index("tile")
    slot_data = strain_elastic[0]
    sub_count = slot_data.shape[0]
    capacity = sub_count // 2
    id_table = strain_ids.reshape(tile_count, sub_count)
    destination = id_table // sub_count
    row_within = id_table % sub_count
    earlier = jnp.arange(sub_count)[:, None] < jnp.arange(sub_count)[None, :]
    matches = destination[:, :, None] == destination[:, None, :]
    rank_table = jnp.sum((matches & earlier[None]).astype(jnp.int32), axis=1)
    my_dest = lax.dynamic_index_in_dim(destination, my_tile, 0, False)
    my_rank = lax.dynamic_index_in_dim(rank_table, my_tile, 0, False)
    slot_index = my_dest * capacity + my_rank
    selector = (jnp.arange(tile_count * capacity)[:, None] == slot_index[None, :]).astype(
        jnp.float32
    )
    outgoing = jnp.dot(selector, slot_data.reshape(sub_count, -1), precision=HIGHEST)
    outgoing = outgoing.reshape(tile_count, capacity, -1)
    incoming = lax.all_to_all(outgoing, "tile", split_axis=0, concat_axis=0, tiled=True)
    hits = (destination == my_tile).astype(jnp.float32)
    row_onehot = (row_within[None, :, :] == jnp.arange(sub_count)[:, None, None]).astype(
        jnp.float32
    )
    rank_onehot = (rank_table[:, :, None] == jnp.arange(capacity)[None, None, :]).astype(
        jnp.float32
    )
    mapping = jnp.einsum("rps,ps,psk->rpk", row_onehot, hits, rank_onehot, precision=HIGHEST)
    gathered = jnp.dot(
        mapping.reshape(sub_count, tile_count * capacity),
        incoming.reshape(tile_count * capacity, -1),
        precision=HIGHEST,
    )
    return jnp.transpose(gathered.reshape(sub_count, 6, -1), (1, 0, 2)).reshape(6, rows, cols)


def couple_cells(amplitude, cross_hop, strain_mix):
    padded_rows = extended(amplitude, (("tile", 4),), 1)
    upward = padded_rows[:, :, :, :, 2:]
    downward = padded_rows[:, :, :, :, :-2]
    widths = [(0, 0)] * 5
    toward_right = jnp.pad(amplitude[..., 1:], widths + [(0, 1)])
    toward_left = jnp.pad(amplitude[..., :-1], widths + [(1, 0)])
    hoppers = jnp.stack([cross_hop[0], cross_hop[0].T, cross_hop[1], cross_hop[1].T])
    nearby = jnp.stack([toward_right, toward_left, upward, downward])
    summed = jnp.einsum("dbc,dktcpyx->ktbpyx", hoppers, nearby, precision=HIGHEST)
    return summed + jnp.einsum("bcyx,ktcpyx->ktbpyx", strain_mix, amplitude, precision=HIGHEST)


def chain_join(earlier, later):
    return (complex_times(earlier[0], later[0]), complex_times(later[0], earlier[1]) + later[1])


def line_end(values, root):
    return from_root(values, "cuts", root)


def sweep_solver(decay_rate, slice_hop, cut_count):
    decay_probe = decay_rate[:, :, :, None]
    bit_count = cut_count.bit_length()
    unit_value = jnp.stack([jnp.ones_like(decay_probe[0]), jnp.zeros_like(decay_probe[0])])
    full_power = complex_power(decay_probe, cut_count, bit_count)
    closing = complex_inverse(unit_value - full_power)
    leading = -decay_probe / slice_hop[:, None, None, None]

    def solve(residual):
        start = (unit_value, jnp.zeros_like(residual))
        carried = prefix_2((decay_probe, residual), "cuts", chain_join, start, False)
        prefix = complex_times(decay_probe, carried[1]) + residual
        last_total = line_end(prefix, cut_count - 1)
        forward = prefix + complex_times(
            complex_times(complex_times(decay_probe, carried[0]), last_total), closing
        )
        returned = prefix_2((decay_probe, forward), "cuts", chain_join, start, True)
        suffix = complex_times(decay_probe, returned[1]) + forward
        first_total = line_end(suffix, 0)
        backward = suffix + complex_times(
            complex_times(complex_times(decay_probe, returned[0]), first_total), closing
        )
        return complex_times(leading, backward)

    return solve


def on_device(
    probes, test_block, band_edge, slice_hop, cross_hop, deform, strain_elastic, strain_ids
):
    amplitude = probes[0]
    testing = test_block[0]
    bands, probe_count, rows, cols = amplitude.shape
    cut_count = lax.axis_size("cuts")
    tile_count = lax.axis_size("tile")
    strain_cells = relayout_strain(strain_elastic, strain_ids, rows, cols)
    symmetric = 0.5 * (deform + jnp.transpose(deform, (0, 2, 1)))
    strain_mix = jnp.einsum("kyx,kbc->bcyx", strain_cells, symmetric, precision=HIGHEST)
    scale = (cut_count * bands * rows * tile_count * cols) ** (-0.5)
    angles = [math.pi * (2 * point + 1) / PTS for point in range(PTS)]
    decay_rate = jnp.stack(
        [line_ratio(band_edge, slice_hop, math.cos(angle), math.sin(angle)) for angle in angles],
        axis=1,
    )
    solver = sweep_solver(decay_rate, slice_hop, cut_count)
    source = jnp.stack([amplitude, jnp.zeros_like(amplitude)])
    source = jnp.broadcast_to(source[:, None], (2, PTS) + amplitude.shape)
    first_step = solver(source)
    second_step = first_step + solver(couple_cells(first_step, cross_hop, strain_mix))
    tested = jnp.einsum("bqyx,ktbryx->ktqr", testing, second_step, precision=HIGHEST)
    weight_re = jnp.asarray(
        np.array(
            [[math.cos((order + 1) * angle) / PTS for angle in angles] for order in range(NMOM)],
            dtype=np.float32,
        )
    )
    weight_im = jnp.asarray(
        np.array(
            [[math.sin((order + 1) * angle) / PTS for angle in angles] for order in range(NMOM)],
            dtype=np.float32,
        )
    )
    projected = jnp.stack(
        [
            jnp.einsum("nt,tqr->nqr", weight_re, tested[0], precision=HIGHEST)
            - jnp.einsum("nt,tqr->nqr", weight_im, tested[1], precision=HIGHEST),
            jnp.einsum("nt,tqr->nqr", weight_re, tested[1], precision=HIGHEST)
            + jnp.einsum("nt,tqr->nqr", weight_im, tested[0], precision=HIGHEST),
        ],
        axis=1,
    )
    fields = jnp.stack(
        [
            jnp.einsum("nt,tbpyx->nbpyx", weight_re[:2], second_step[0], precision=HIGHEST)
            - jnp.einsum("nt,tbpyx->nbpyx", weight_im[:2], second_step[1], precision=HIGHEST),
            jnp.einsum("nt,tbpyx->nbpyx", weight_re[:2], second_step[1], precision=HIGHEST)
            + jnp.einsum("nt,tbpyx->nbpyx", weight_im[:2], second_step[0], precision=HIGHEST),
        ],
        axis=1,
    )
    projected = lax.psum(projected * scale, ("cuts", "tile"))
    return (fields[:, :, None], projected)


def solution(mesh):
    placed = (
        P("cuts", None, None, "tile", None),
        P("cuts", None, None, "tile", None),
        P(None, "tile", None),
        P(),
        P(),
        P(),
        P("cuts", "tile", None, None),
        P(),
    )
    return jax.shard_map(
        on_device,
        mesh=mesh,
        in_specs=placed,
        out_specs=(P(None, None, "cuts", None, None, "tile", None), P()),
        check_vma=False,
    )
```

profile of v0, /device:TPU:1, one launch (start us, length us, event | category | flops | bytes accessed | tf_op | source)
XLA Modules:
  0.0 1907.6 jit_solution(2123157860716774347)
XLA Ops:
  12.9 45.3 %all-gather.12.cloned.1.call-done = f32[64,8,8,1,128]{4,2,3,1,0:T(8,128)} async-done(((f32[2,8,8,1,128]{4,2,3,1,0:T(8,128)}), f32[64,8,8,1,128]{4,2,3,1,0:T(8,128)}) %all-gather.12.cloned.1.call-update) | async-done | bytes 2097168 | tf_op jit(solution)/shard_map/all_gather | solution.py:36
  58.2 48.1 %all-gather.14.cloned.1.call-done = f32[64,8,16,1,128]{4,2,3,1,0:T(8,128)} async-done(((f32[2,8,16,1,128]{4,2,3,1,0:T(8,128)}), f32[64,8,16,1,128]{4,2,3,1,0:T(8,128)}) %all-gather.14.cloned.1.call-update) | async-done | bytes 4194320 | tf_op jit(solution)/shard_map/all_gather | solution.py:36
  106.3 12.7 broadcast.586
  119.0 220.5 %while.68 = (s32[]{:T(128)}, f32[2,8,8,1,1,128]{5,4,3,2,1,0:T(1,128)S(1)}, f32[2,8,8,16,1,128]{5,4,3,2,1,0:T(1,128)S(1)}, s32[]{:T(128)}, f32[32,2,8,8,1,1,128]{...) while((s32[]{:T(128)}, ...), condition=%wide.region_1.2_spmd.clone, body=%wide.region_0.1_spmd.clone.sunk | while | flops 2179077 | bytes 11075731 | solution.py:49
  123.5 2.4 broadcast_select_fusion.29
  130.4 2.4 broadcast_select_fusion.29
  137.3 2.4 broadcast_select_fusion.29
  144.2 2.4 broadcast_select_fusion.29
  151.1 2.4 broadcast_select_fusion.29
  158.0 2.4 broadcast_select_fusion.29
  247.6 2.4 broadcast_select_fusion.29
  254.4 2.4 broadcast_select_fusion.29
  261.3 2.4 broadcast_select_fusion.29
  268.2 2.4 broadcast_select_fusion.29
  275.1 2.4 broadcast_select_fusion.29
  282.0 2.4 broadcast_select_fusion.29
  288.9 2.4 broadcast_select_fusion.29
  341.4 103.5 %all-reduce.8.cloned.1.call-done = f32[2,8,8,16,1,128]{5,2,3,1,4,0:T(8,128)} async-done(((f32[2,8,8,16,1,128]{5,2,3,1,4,0:T(8,128)}), f32[2,8,8,16,1,128]{5,2,3,1,4,0:T(8,128)}) %all-reduce.8.cloned.1.call-update) | async-done | bytes 1048592 | tf_op jit(solution)/shard_map/psum | solution.py:31
  449.5 4.1 all-to-all-start
  461.2 100.6 %all-gather.10.cloned.1.call-done = f32[32,2,8,8,16,1,128]{6,4,5,3,2,1,0:T(8,128)} async-done(((f32[1,2,8,8,16,1,128]{6,4,5,3,2,1,0:T(8,128)}), f32[32,2,8,8,16,1,128]{6,4,5,3,2,1,0:T(8,128)}) %all-gather.10.cloned.1.call-update) | async-done | bytes 33554448 | tf_op jit(solution)/shard_map/all_gather | solution.py:36
  561.8 220.6 %while.69 = (s32[]{:T(128)}, f32[2,8,8,1,1,128]{5,4,3,2,1,0:T(1,128)S(1)}, f32[2,8,8,16,1,128]{5,4,3,2,1,0:T(1,128)S(1)}, s32[]{:T(128)}, f32[32,2,8,8,1,1,128]{...) while((s32[]{:T(128)}, ...), condition=%wide.region_4.5_spmd.clone, body=%wide.region_3.4_spmd.clone.sunk | while | flops 2179081 | bytes 11075793 | solution.py:49
  593.8 2.4 broadcast_select_fusion.32
  600.7 2.4 broadcast_select_fusion.32
  635.2 2.4 broadcast_select_fusion.32
  642.0 2.4 broadcast_select_fusion.32
  676.5 2.4 broadcast_select_fusion.32
  683.4 2.4 broadcast_select_fusion.32
  690.3 2.4 broadcast_select_fusion.32
  724.8 2.4 broadcast_select_fusion.32
  731.7 2.4 broadcast_select_fusion.32
  766.2 2.4 broadcast_select_fusion.32
  773.0 2.4 broadcast_select_fusion.32
  787.6 101.2 %all-reduce.10.cloned.1.call-done = f32[2,8,8,16,1,128]{5,2,3,1,4,0:T(8,128)} async-done(((f32[2,8,8,16,1,128]{5,2,3,1,4,0:T(8,128)}), f32[2,8,8,16,1,128]{5,2,3,1,4,0:T(8,128)}) %all-reduce.10.cloned.1.call-update) | async-done | bytes 1048592 | tf_op jit(solution)/shard_map/psum | solution.py:31
  895.0 4.6 collective-permute-start.1
  900.9 7.5 copy.296
  908.4 11.6 fusion.59
  919.9 7.5 copy.298
  928.3 4.1 fusion.8
  933.8 114.6 %all-gather.16.cloned.1.call-done = f32[64,8,8,16,1,128]{5,3,4,2,1,0:T(8,128)} async-done(((f32[2,8,8,16,1,128]{5,3,4,2,1,0:T(8,128)}), f32[64,8,8,16,1,128]{5,3,4,2,1,0:T(8,128)}) %all-gather.16.cloned.1.call-update) | async-done | bytes 33554448 | tf_op jit(solution)/shard_map/all_gather | solution.py:36
  1048.5 220.5 %while.70 = (s32[]{:T(128)}, f32[2,8,8,1,1,128]{5,4,3,2,1,0:T(1,128)S(1)}, f32[2,8,8,16,1,128]{5,4,3,2,1,0:T(1,128)S(1)}, s32[]{:T(128)}, f32[32,2,8,8,1,1,128]{...) while((s32[]{:T(128)}, ...), condition=%wide.region_8.9_spmd.clone, body=%wide.region_7.8_spmd.clone.sunk | while | flops 2179077 | bytes 11075731 | solution.py:49
  1135.6 2.4 broadcast_select_fusion.35
  1142.5 2.4 broadcast_select_fusion.35
  1149.4 2.4 broadcast_select_fusion.35
  1156.3 2.4 broadcast_select_fusion.35
  1163.2 2.4 broadcast_select_fusion.35
  1170.1 2.4 broadcast_select_fusion.35
  1177.0 2.4 broadcast_select_fusion.35
  1266.6 2.4 broadcast_select_fusion.35
  1270.7 103.5 %all-reduce.12.cloned.1.call-done = f32[2,8,8,16,1,128]{5,2,3,1,4,0:T(8,128)} async-done(((f32[2,8,8,16,1,128]{5,2,3,1,4,0:T(8,128)}), f32[2,8,8,16,1,128]{5,2,3,1,4,0:T(8,128)}) %all-reduce.12.cloned.1.call-update) | async-done | bytes 1048592 | tf_op jit(solution)/shard_map/psum | solution.py:31
  1378.0 114.0 %all-gather.18.cloned.1.call-done = f32[64,8,8,16,1,128]{5,3,4,2,1,0:T(8,128)} async-done(((f32[2,8,8,16,1,128]{5,3,4,2,1,0:T(8,128)}), f32[64,8,8,16,1,128]{5,3,4,2,1,0:T(8,128)}) %all-gather.18.cloned.1.call-update) | async-done | bytes 33554448 | tf_op jit(solution)/shard_map/all_gather | solution.py:36
  1492.0 220.6 %while.71 = (s32[]{:T(128)}, f32[2,8,8,1,1,128]{5,4,3,2,1,0:T(1,128)S(1)}, f32[2,8,8,16,1,128]{5,4,3,2,1,0:T(1,128)S(1)}, s32[]{:T(128)}, f32[32,2,8,8,1,1,128]{...) while((s32[]{:T(128)}, ...), condition=%wide.region_11.12_spmd.clone, body=%wide.region_10.11_spmd.clone.sunk | while | flops 2179081 | bytes 11075793 | solution.py:49
  1496.5 2.4 broadcast_select_fusion.38
  1510.3 2.4 broadcast_select_fusion.38
  1524.0 2.4 broadcast_select_fusion.38
  1572.3 2.4 broadcast_select_fusion.38
  1586.1 2.4 broadcast_select_fusion.38
  1599.9 2.4 broadcast_select_fusion.38
  1613.7 2.4 broadcast_select_fusion.38
  1627.5 2.4 broadcast_select_fusion.38
  1641.2 2.4 broadcast_select_fusion.38
  1655.0 2.4 broadcast_select_fusion.38
  1714.1 2.5 broadcast_select_fusion.14
  1716.6 103.6 %all-reduce.14.cloned.1.call-done = f32[2,8,8,16,1,128]{5,2,3,1,4,0:T(8,128)} async-done(((f32[2,8,8,16,1,128]{5,2,3,1,4,0:T(8,128)}), f32[2,8,8,16,1,128]{5,2,3,1,4,0:T(8,128)}) %all-reduce.14.cloned.1.call-update) | async-done | bytes 1048592 | tf_op jit(solution)/shard_map/psum | solution.py:31
  1829.4 66.1 %psum.39 = f32[4,2,16,16]{3,0,2,1:T(4,128)S(1)} all-reduce(f32[4,2,16,16]{3,0,2,1:T(4,128)S(1)} %maximum_multiply_fusion), channel_id=1, replica_groups=mesh['cuts'=32,'tile'=4] {'cuts','tile'}, use_global_device_ids=true, to_apply=%region_13.14 | all-reduce | flops 2048 | bytes 16384 | tf_op jit(solution)/shard_map/psum | solution.py:237
  (1040 shorter events, 828.8 us)
Async XLA Ops:
  7.2 1818.9 %copy-start = (f32[1,8,16,1,128]{4,3,2,1,0:T(1,128)S(1)}, f32[1,8,16,1,128]{4,3,2,1,0:T(1,128)}, u32[]{:S(2)}) copy-start(f32[1,8,16,1,128]{4,3,2,1,0:T(1,128)} %param.19) | copy-start | bytes 196612
  7.2 51.0 %all-gather.12.cloned.1.call-start = ((), (), s32[]{:S(2)}) async-start(), calls=%async_computation.6 | async-start | bytes 2162688 | tf_op jit(solution)/shard_map/all_gather | solution.py:36
  8.2 0.6 copy-start.9
  8.8 97.4 %all-gather.14.cloned.1.call-start = ((), (), s32[]{:S(2)}) async-start(), calls=%async_computation.7 | async-start | bytes 4325376 | tf_op jit(solution)/shard_map/all_gather | solution.py:36
  10.4 434.5 %all-reduce.8.cloned.1.call-start = ((), (), s32[]{:S(2)}) async-start(), calls=%async_computation.1 | async-start | bytes 2097152 | tf_op jit(solution)/shard_map/psum | solution.py:31
  12.1 327.8 %copy-start.11 = (f32[8,8,128]{2,1,0:T(8,128)}, f32[8,8,128]{2,1,0:T(8,128)S(1)}, u32[]{:S(2)}) copy-start(f32[8,8,128]{2,1,0:T(8,128)S(1)} %slice_bitcast_fusion.15) | copy-start | bytes 98308
  12.9 327.0 %copy-start.13 = (f32[8,8,128]{2,1,0:T(8,128)}, f32[8,8,128]{2,1,0:T(8,128)S(1)}, u32[]{:S(2)}) copy-start(f32[8,8,128]{2,1,0:T(8,128)S(1)} %slice_bitcast_fusion.16) | copy-start | bytes 98308
  119.0 222.2 %copy-start.10 = (f32[2,8,8,1,128]{4,2,3,1,0:T(8,128)S(1)}, f32[2,8,8,1,128]{4,2,3,1,0:T(8,128)}, u32[]{:S(2)}) copy-start(f32[2,8,8,1,128]{4,2,3,1,0:T(8,128)} %copy-done.9) | copy-start | bytes 196612
  119.0 222.3 %copy-start.21 = (f32[2,8,8,1,1,128]{5,2,1,4,3,0:T(8,128)S(1)}, f32[2,8,8,1,1,128]{5,2,1,4,3,0:T(8,128)}, u32[]{:S(2)}) copy-start(f32[2,8,8,1,1,128]{5,2,1,4,3,0:T(8,128)} %constant.221.clone.1) | copy-start | bytes 196612
  339.6 108.8 %copy-start.22 = (f32[1,4,6,32]{3,1,2,0:T(4,128)S(1)}, f32[1,4,6,32]{3,1,2,0:T(4,128)}, u32[]{:S(2)}) copy-start(f32[1,4,6,32]{3,1,2,0:T(4,128)} %param.24) | copy-start | bytes 9220
  341.2 220.6 %all-gather.10.cloned.1.call-start = ((), (), s32[]{:S(2)}) async-start(), calls=%async_computation.2 | async-start | bytes 34603008 | tf_op jit(solution)/shard_map/all_gather | solution.py:36
  341.4 105.0 %copy-start.15 = (f32[8,8,128]{2,1,0:T(8,128)}, f32[8,8,128]{2,1,0:T(8,128)S(1)}, u32[]{:S(2)}) copy-start(f32[8,8,128]{2,1,0:T(8,128)S(1)} %get-tuple-element.848) | copy-start | bytes 98308
  341.4 105.0 %copy-start.17 = (f32[8,8,128]{2,1,0:T(8,128)}, f32[8,8,128]{2,1,0:T(8,128)S(1)}, u32[]{:S(2)}) copy-start(f32[8,8,128]{2,1,0:T(8,128)S(1)} %get-tuple-element.849) | copy-start | bytes 98308
  449.5 11.0 all-to-all-start
  453.6 435.2 %all-reduce.10.cloned.1.call-start = ((), (), s32[]{:S(2)}) async-start(), calls=%async_computation.3 | async-start | bytes 2097152 | tf_op jit(solution)/shard_map/psum | solution.py:31
  782.4 2.9 copy-start.27
  785.2 263.2 %all-gather.16.cloned.1.call-start = ((), (), s32[]{:S(2)}) async-start(), calls=%async_computation.8 | async-start | bytes 34603008 | tf_op jit(solution)/shard_map/all_gather | solution.py:36
  893.6 33.8 %copy-start.1 = (f32[1,8,8,16,1,128]{5,2,3,1,0,4:T(8,128)}, f32[1,8,8,16,1,128]{5,2,3,1,0,4:T(8,128)S(1)}, u32[]{:S(2)}) copy-start(f32[1,8,8,16,1,128]{5,2,3,1,0,4:T(8,128)S(1)} %get-tuple-element.816) | copy-start | bytes 1572868
  893.6 33.8 %copy-start.3 = (f32[1,8,8,16,1,128]{5,2,3,1,0,4:T(8,128)}, f32[1,8,8,16,1,128]{5,2,3,1,0,4:T(8,128)S(1)}, u32[]{:S(2)}) copy-start(f32[1,8,8,16,1,128]{5,2,3,1,0,4:T(8,128)S(1)} %get-tuple-element.817) | copy-start | bytes 1572868
  895.0 33.2 %collective-permute-start.1 = (f32[2,8,8,16,1,128]{5,2,3,1,0,4:T(8,128)}, f32[2,8,8,16,1,128]{5,2,3,1,0,4:T(8,128)}, u32[]{:S(2)}, u32[]{:S(2)}) collective-permute-start(f32[2,8,8,16,1,128]{5,2,3,1,0,4:T(8,128)} %get-tuple-element.829), channel_id=1, source_target_pairs={{0,1},{1,2},{2,3},{4,5},{5,6},{6,7},{8,9},{9,10},{10,11},{12,13},{... | collective-permute-start | bytes 3145736 | tf_op jit(solution)/shard_map/ppermute | solution.py:21
  899.6 28.6 %collective-permute-start = (f32[2,8,8,16,1,128]{5,2,3,1,0,4:T(8,128)}, f32[2,8,8,16,1,128]{5,2,3,1,0,4:T(8,128)}, u32[]{:S(2)}, u32[]{:S(2)}) collective-permute-start(f32[2,8,8,16,1,128]{5,2,3,1,0,4:T(8,128)} %get-tuple-element.829), channel_id=1, source_target_pairs={{1,0},{2,1},{3,2},{5,4},{6,5},{7,6},{9,8},{10,9},{11,10},{13,12},{... | collective-permute-start | bytes 3145736 | tf_op jit(solution)/shard_map/ppermute | solution.py:24
  919.9 8.3 copy-start.28
  919.9 8.3 copy-start.29
  919.9 8.3 copy-start.30
  919.9 8.3 copy-start.31
  933.6 440.7 %all-reduce.12.cloned.1.call-start = ((), (), s32[]{:S(2)}) async-start(), calls=%async_computation.4 | async-start | bytes 2097152 | tf_op jit(solution)/shard_map/psum | solution.py:31
  1048.5 220.9 %copy-start.12 = (f32[8,8,128]{2,1,0:T(8,128)S(1)}, f32[8,8,128]{2,1,0:T(8,128)}, u32[]{:S(2)}) copy-start(f32[8,8,128]{2,1,0:T(8,128)} %copy-done.11) | copy-start | bytes 98308
  1048.5 220.9 %copy-start.14 = (f32[8,8,128]{2,1,0:T(8,128)S(1)}, f32[8,8,128]{2,1,0:T(8,128)}, u32[]{:S(2)}) copy-start(f32[8,8,128]{2,1,0:T(8,128)} %copy-done.13) | copy-start | bytes 98308
  1269.0 105.3 %copy-start.16 = (f32[8,8,128]{2,1,0:T(8,128)S(1)}, f32[8,8,128]{2,1,0:T(8,128)}, u32[]{:S(2)}) copy-start(f32[8,8,128]{2,1,0:T(8,128)} %copy-done.15) | copy-start | bytes 98308
  1269.0 105.3 %copy-start.18 = (f32[8,8,128]{2,1,0:T(8,128)S(1)}, f32[8,8,128]{2,1,0:T(8,128)}, u32[]{:S(2)}) copy-start(f32[8,8,128]{2,1,0:T(8,128)} %copy-done.17) | copy-start | bytes 98308
  1270.7 221.4 %all-gather.18.cloned.1.call-start = ((), (), s32[]{:S(2)}) async-start(), calls=%async_computation.9 | async-start | bytes 34603008 | tf_op jit(solution)/shard_map/all_gather | solution.py:36
  1375.7 0.8 copy-start.5
  1375.7 1.0 copy-start.6
  1377.9 442.3 %all-reduce.14.cloned.1.call-start = ((), (), s32[]{:S(2)}) async-start(), calls=%async_computation.5 | async-start | bytes 2097152 | tf_op jit(solution)/shard_map/psum | solution.py:31
  1713.0 110.7 %copy-start.19 = (f32[8,8,128]{2,1,0:T(8,128)S(1)}, f32[8,8,128]{2,1,0:T(8,128)}, u32[]{:S(2)}) copy-start(f32[8,8,128]{2,1,0:T(8,128)} %get-tuple-element.844) | copy-start | bytes 98308
  1713.0 110.7 %copy-start.20 = (f32[8,8,128]{2,1,0:T(8,128)S(1)}, f32[8,8,128]{2,1,0:T(8,128)}, u32[]{:S(2)}) copy-start(f32[8,8,128]{2,1,0:T(8,128)} %get-tuple-element.845) | copy-start | bytes 98308
  1713.1 0.8 copy-start.7
  1713.1 1.0 copy-start.8
  1821.6 5.6 copy-start.2
  1821.6 5.6 copy-start.4
  1823.7 4.9 copy-start.24
  1823.7 5.3 copy-start.23
  1823.7 72.5 %copy-start.26 = (f32[2,8,1,1]{1,0,3,2:T(2,128)S(1)}, f32[2,8,1,1]{1,0,3,2:T(2,128)}, u32[]{:S(2)}) copy-start(f32[2,8,1,1]{1,0,3,2:T(2,128)} %constant.247) | copy-start | bytes 196
  1823.8 74.1 %copy-start.25 = (f32[2,8,1,1]{1,0,3,2:T(2,128)S(1)}, f32[2,8,1,1]{1,0,3,2:T(2,128)}, u32[]{:S(2)}) copy-start(f32[2,8,1,1]{1,0,3,2:T(2,128)} %constant.248) | copy-start | bytes 196
Sparse Core Ops, SparseCore 0:
  10.8 47.3 all-gather.11
  61.1 45.1 all-gather.13
  341.3 103.5 all-reduce.7
  447.8 113.9 all-gather.9
  785.3 103.4 all-reduce.9
  933.7 114.7 all-gather.15
  1270.8 103.4 all-reduce.11
  1378.1 113.9 all-gather.17
  1716.7 103.4 all-reduce.13
where the time goes:
time: 1930 us; the launch traced here: 1910 us
  waiting for transfers between devices  835 us (43%)
  other arithmetic  633 us (33%)
  local copies, waits for them, and re-layouts  317 us (16%)
  blocking collectives  66.1 us (3%)
  matrix products  24.3 us (1%)
    all_gather x5, waiting for transfers between devices, prefix_2(): everything = jax.tree.map(lambda part: lax.all_gather(part, axis), array)  423 us
    psum x4, waiting for transfers between devices, from_root(): return lax.psum(jnp.where(mine, array, jnp.zeros_like(array)), axis)  412 us
    select_n x256, other arithmetic, hop(): return jax.tree.map(lambda a, b: jnp.where(reached, a, b), new, before)  324 us
    dynamic_slice x128, local copies, waits for them, and re-layouts, hop(): new = combine(before, jax.tree.map(lambda part: part[at], everything))  169 us
    sub x267, other arithmetic, complex_times(): former[0] * latter[0] - former[1] * latter[1]  157 us
    while x128, other arithmetic  131 us
    slice x128, local copies, waits for them, and re-layouts, complex_times(): latter[1]  101 us
    psum x1, blocking collectives, on_device(): projected = lax.psum(projected * scale, ('cuts', 'tile'))  66.1 us
  transfers between devices with their start and end apart: 12, of which 9 were waited for; matrix products, arithmetic and copies ran while one was open for 2% of the time, Pallas kernels for 0%

commit v1 on v0

v1 whole, which is shorter than its diff:
```python
import math

import jax
import jax.numpy as jnp
import numpy as np
from jax import lax
from jax.experimental import pallas as pl
from jax.experimental.pallas import tpu as pltpu
from jax.sharding import PartitionSpec as P

PTS = 8
NMOM = 4
HALF = PTS // 2
ALL = ("cuts", "tile")

BANDS = 8
CELLS = 128
ROWS = 4
SLICES = 32
PROBES = 16
STRAINS = 6
TERMS = STRAINS + 4
PLANE = ROWS * CELLS
DEVICES = SLICES * ROWS
CHUNK = 20
BACK = 4
NSUB = ROWS * ROWS
HIGHEST = lax.Precision.HIGHEST
VMEM_BYTES = 20 * 1024 * 1024


def pack_kernel(ids_ref, probes_ref, test_ref, strain_ref, edge_ref, out_ref):
    piece = lax.axis_index("cuts") % BANDS
    edge = edge_ref[pl.ds(piece, 1), :]
    strain = jnp.concatenate([strain_ref[:, slot, :] for slot in range(ROWS)], axis=1)
    shared = [
        jnp.concatenate([strain[3 * half : 3 * half + 3], edge], axis=0) for half in range(2)
    ]
    for probe in range(PROBES):
        half = probe // 4 % 2
        column = probes_ref[pl.ds(probe, BANDS, stride=PROBES), :]
        for band in range(BANDS):
            at = (band * PROBES + probe) * CHUNK
            out_ref[at : at + 8, :] = column
            out_ref[at + 8 : at + 12, :] = shared[half]
            first = band * PROBES + 8 * half
            out_ref[at + 12 : at + 20, :] = test_ref[first : first + 8, :]


def split(value):
    high = value.astype(jnp.bfloat16)
    low = (value - high.astype(jnp.float32)).astype(jnp.bfloat16)
    return high, low


def matmul(left, right):
    return jnp.dot(left, right, preferred_element_type=jnp.float32)


def main_kernel(
    scale,
    cosines,
    ids_ref,
    hop_ref,
    cross_ref,
    deform_ref,
    table_ref,
    mine_ref,
    other_ref,
    wave_ref,
    spread_ref,
    forth_ref,
    back_ref,
    cosine_ref,
    out_ref,
    place_ref,
    slots_ref,
    strain_ref,
    weights_ref,
    right_ref,
    waves_ref,
    field_ref,
    result_ref,
    source_ref,
    moment_ref,
    final_ref,
):
    half = lax.axis_index("cuts") % 2
    band = lax.axis_index("cuts") // 4
    lane = lax.broadcasted_iota(jnp.int32, (SLICES, CELLS), 1)

    for slot in range(NSUB):
        place_ref[ids_ref[slot]] = slot
    for holder in range(ROWS):
        for comp in range(3):
            rows = pl.ds(holder * CHUNK + 8 + comp, SLICES, stride=ROWS * CHUNK)
            a = mine_ref[rows, :]
            b = other_ref[rows, :]
            slots_ref[holder, comp * SLICES : (comp + 1) * SLICES, :] = jnp.where(half == 0, a, b)
            slots_ref[holder, (comp + 3) * SLICES : (comp + 4) * SLICES, :] = jnp.where(
                half == 0, b, a
            )
    group = lax.broadcasted_iota(jnp.int32, (STRAINS * SLICES, CELLS), 1) // (CELLS // ROWS)
    for row in range(ROWS):
        total = None
        for part in range(ROWS):
            slot = place_ref[row * ROWS + part]
            shift = ((part + ROWS - slot % ROWS) % ROWS) * (CELLS // ROWS)
            rolled = pltpu.roll(slots_ref[slot // ROWS], shift, 1)
            total = rolled if total is None else jnp.where(group == part, rolled, total)
        strain_ref[:, row * CELLS : (row + 1) * CELLS] = total

    source_band = lax.broadcasted_iota(jnp.int32, (1, SLICES * BANDS), 1) % BANDS
    for term in range(TERMS):
        line = jnp.zeros((1, SLICES * BANDS), jnp.float32)
        for src in range(BANDS):
            if term < STRAINS:
                entry = 0.5 * (deform_ref[term, band, src] + deform_ref[term, src, band])
            else:
                axis = (term - STRAINS) // 2
                if (term - STRAINS) % 2 == 0:
                    entry = cross_ref[axis, band, src]
                else:
                    entry = cross_ref[axis, src, band]
            line = jnp.where(source_band == src, entry, line)
        high, low = split(spread_ref[...] * line)
        at = slice(term * SLICES, (term + 1) * SLICES)
        weights_ref[at, 0:256] = high
        weights_ref[at, 256:512] = high
        weights_ref[at, 512:768] = low

    for s in range(SLICES):
        for row in range(ROWS):
            at = (s * ROWS + row) * CHUNK
            field_ref[s * BANDS : (s + 1) * BANDS, row * CELLS : (row + 1) * CELLS] = mine_ref[
                at : at + BANDS, :
            ]
    high, low = split(field_ref[:, 0:PLANE])
    right_ref[0:256, 0:PLANE] = high
    right_ref[256:512, 0:PLANE] = low
    right_ref[512:768, 0:PLANE] = high
    waves = matmul(wave_ref[...], right_ref[:, 0:PLANE])
    for row in range(ROWS):
        waves_ref[row] = waves[:, row * CELLS : (row + 1) * CELLS]

    sub = lax.broadcasted_iota(jnp.int32, (BANDS, CELLS), 0)
    hop = jnp.full((BANDS, CELLS), 2.0 * hop_ref[0], jnp.float32)
    for b in range(1, BANDS):
        hop = jnp.where(sub == b, 2.0 * hop_ref[b], hop)
    own_hop = 2.0 * hop_ref[band]
    moment_ref[...] = jnp.zeros_like(moment_ref)

    def point(j, _):
        z_re = table_ref[0, j]
        z_im = table_ref[1, j]
        square = z_im * z_im
        for row in range(ROWS):
            lanes = slice(row * CELLS, (row + 1) * CELLS)
            lanes_im = slice(PLANE + row * CELLS, PLANE + (row + 1) * CELLS)
            gap = z_re - mine_ref[pl.ds(row * CHUNK + 11, BANDS, stride=ROWS * CHUNK), :]
            for freq in range(SLICES // 2 + 1):
                u = gap + hop * cosines[freq]
                inverse = 1.0 / (u * u + square)
                g_re = u * inverse
                g_im = -z_im * inverse
                both = (freq, freq + SLICES // 2) if 0 < freq < SLICES // 2 else (freq,)
                for wave in both:
                    at = slice(wave * BANDS, (wave + 1) * BANDS)
                    value = waves_ref[row, at, :]
                    field_ref[at, lanes] = g_re * value
                    field_ref[at, lanes_im] = g_im * value
        high, low = split(field_ref[...])
        right_ref[0:256, :] = high
        right_ref[256:512, :] = low
        right_ref[512:768, :] = high
        result_ref[...] = matmul(weights_ref[...], right_ref[...])

        for part in range(2):
            for row in range(ROWS):
                at = part * PLANE + row * CELLS
                lanes = slice(at, at + CELLS)
                total = None
                for comp in range(STRAINS):
                    rows = slice(comp * SLICES, (comp + 1) * SLICES)
                    value = strain_ref[rows, row * CELLS : (row + 1) * CELLS] * result_ref[
                        rows, lanes
                    ]
                    total = value if total is None else total + value
                from_right = pltpu.roll(result_ref[192:224, lanes], CELLS - 1, 1)
                from_left = pltpu.roll(result_ref[224:256, lanes], 1, 1)
                total = total + jnp.where(lane < CELLS - 1, from_right, 0.0)
                total = total + jnp.where(lane > 0, from_left, 0.0)
                if row < ROWS - 1:
                    total = total + result_ref[256:288, at + CELLS : at + 2 * CELLS]
                if row > 0:
                    total = total + result_ref[288:320, at - CELLS : at]
                high, low = split(total)
                source_ref[0:32, lanes] = high
                source_ref[32:64, lanes] = low
                source_ref[64:96, lanes] = high
        result_ref[0:32, :] = matmul(forth_ref[...], source_ref[:, 0 : 2 * PLANE])

        for row in range(ROWS):
            lanes = slice(row * CELLS, (row + 1) * CELLS)
            lanes_im = slice(PLANE + row * CELLS, PLANE + (row + 1) * CELLS)
            edge = mine_ref[pl.ds((band * ROWS + row) * CHUNK + 11, 1), :]
            u = (z_re - edge) + own_hop * cosine_ref[...]
            inverse = 1.0 / (u * u + square)
            g_re = u * inverse
            g_im = -z_im * inverse
            a_re = result_ref[0:32, lanes] + waves_ref[row, pl.ds(band, SLICES, stride=BANDS), :]
            a_im = result_ref[0:32, lanes_im]
            v_re = g_re * a_re - g_im * a_im
            v_im = g_re * a_im + g_im * a_re
            for order in range(NMOM):
                at = slice(order * PLANE + row * CELLS, order * PLANE + (row + 1) * CELLS)
                moment_ref[:, at] += (
                    table_ref[2 + order, j] * v_re - table_ref[2 + NMOM + order, j] * v_im
                )
        return 0

    lax.fori_loop(0, HALF, point, 0)

    high, low = split(moment_ref[...])
    source_ref[0:32, :] = high
    source_ref[32:64, :] = low
    source_ref[64:96, :] = high
    final = matmul(back_ref[...], source_ref[...])
    for order in range(NMOM):
        for row in range(ROWS):
            at = order * PLANE + row * CELLS
            value = final[:, at : at + CELLS]
            final_ref[order * ROWS + row] = value
            if order < 2:
                out_ref[pl.ds(row * BACK + order, SLICES, stride=ROWS * BACK), :] = value

    zero = jnp.zeros((8, CELLS), jnp.float32)
    near = [zero] * NMOM
    far = [zero] * NMOM
    for s in range(SLICES):
        for row in range(ROWS):
            at = (s * ROWS + row) * CHUNK + 12
            test_near = mine_ref[at : at + 8, :]
            test_far = other_ref[at : at + 8, :]
            for order in range(NMOM):
                value = final_ref[order * ROWS + row, s : s + 1, :]
                near[order] = near[order] + test_near * value
                far[order] = far[order] + test_far * value
    stack = []
    for order in range(NMOM):
        stack.append(jnp.where(half == 0, near[order], far[order]))
        stack.append(jnp.where(half == 0, far[order], near[order]))
    sums = lax.dot_general(
        jnp.full((8, CELLS), scale, jnp.float32),
        jnp.concatenate(stack, axis=0),
        (((1,), (1,)), ((), ())),
        precision=HIGHEST,
        preferred_element_type=jnp.float32,
    )
    line = jnp.concatenate([sums, jnp.zeros_like(sums)], axis=1)[0:1]
    out_ref[pl.ds(2, DEVICES, stride=BACK), :] = jnp.broadcast_to(line, (DEVICES, CELLS))


def gather_kernel(blocks_ref, fields_ref, projected_ref):
    total = None
    for band in range(BANDS):
        first = band * PROBES * BACK
        for order in range(2):
            fields_ref[order, 0, band * PROBES : (band + 1) * PROBES, :] = blocks_ref[
                pl.ds(first + order, PROBES, stride=BACK), :
            ]
        part = blocks_ref[pl.ds(first + 2, PROBES, stride=BACK), :]
        total = part if total is None else total + part
    turned = total.T
    for order in range(2):
        fields_ref[order, 1] = jnp.zeros((BANDS * PROBES, CELLS), jnp.float32)
    for order in range(NMOM):
        projected_ref[order, 0] = turned[order * PROBES : (order + 1) * PROBES, :]
        projected_ref[order, 1] = jnp.zeros((PROBES, PROBES), jnp.float32)


def transform():
    s = np.arange(SLICES)
    rows = []
    for freq in range(SLICES // 2 + 1):
        norm = 1.0 if freq in (0, SLICES // 2) else 2.0
        rows.append(np.sqrt(norm / SLICES) * np.cos(2 * np.pi * freq * s / SLICES))
    for freq in range(1, SLICES // 2):
        rows.append(np.sqrt(2.0 / SLICES) * np.sin(2 * np.pi * freq * s / SLICES))
    return np.array(rows)


def split_constant(matrix):
    matrix = matrix.astype(np.float32)
    high = matrix.astype(jnp.bfloat16)
    low = (matrix - high.astype(np.float32)).astype(jnp.bfloat16)
    return jnp.asarray(np.concatenate([high, high, low], axis=1))


def constants():
    wave = transform()
    freqs = np.concatenate([np.arange(SLICES // 2 + 1), np.arange(1, SLICES // 2)])
    cosine = np.cos(2 * np.pi * freqs / SLICES)
    spread = np.repeat(wave.T, BANDS, axis=1)
    angles = np.pi * (2 * np.arange(HALF) + 1) / PTS
    orders = np.arange(1, NMOM + 1)[:, None]
    table = np.concatenate(
        [
            np.cos(angles)[None],
            np.sin(angles)[None],
            2.0 / PTS * np.cos(orders * angles),
            2.0 / PTS * np.sin(orders * angles),
        ]
    )
    return (
        [float(c) for c in cosine],
        jnp.asarray(table, jnp.float32),
        split_constant(np.kron(wave, np.eye(BANDS))),
        jnp.asarray(spread, jnp.float32),
        split_constant(wave),
        split_constant(wave.T),
        jnp.asarray(np.repeat(cosine[:, None], CELLS, axis=1), jnp.float32),
    )


def vmem():
    return pl.BlockSpec(memory_space=pltpu.VMEM)


def smem():
    return pl.BlockSpec(memory_space=pltpu.SMEM)


def shape(*dims):
    return jax.ShapeDtypeStruct(dims, jnp.float32)


def params():
    return pltpu.CompilerParams(vmem_limit_bytes=VMEM_BYTES)


def exchange(blocks, rows):
    wide = blocks.reshape(DEVICES, rows // 4, 4, CELLS)
    wide = lax.all_to_all(wide, ALL, split_axis=0, concat_axis=0, tiled=True)
    return wide.reshape(DEVICES * rows, CELLS)


def on_device(
    probes, test_block, band_edge, slice_hop, cross_hop, deform, strain_elastic, strain_ids
):
    cut_count = lax.axis_size("cuts")
    outgoing = pl.pallas_call(
        pack_kernel,
        out_shape=shape(DEVICES * CHUNK, CELLS),
        in_specs=[smem()] + [vmem()] * 4,
        out_specs=vmem(),
        compiler_params=params(),
        name="pack",
    )(
        strain_ids,
        probes.reshape(BANDS * PROBES, CELLS),
        test_block.reshape(BANDS * PROBES, CELLS),
        jnp.transpose(strain_elastic[0], (1, 0, 2)),
        band_edge.reshape(BANDS, CELLS),
    )
    mine = exchange(outgoing, CHUNK)
    other = lax.ppermute(mine, "cuts", [(i, i ^ 1) for i in range(cut_count)])
    scale = (cut_count * BANDS * ROWS * CELLS) ** (-0.5)
    cosines, table, *matrices = constants()

    def main(*refs):
        main_kernel(scale, cosines, *refs)

    blocks = pl.pallas_call(
        main,
        out_shape=shape(DEVICES * BACK, CELLS),
        in_specs=[smem()] * 5 + [vmem()] * 7,
        out_specs=vmem(),
        scratch_shapes=[
            pltpu.SMEM((NSUB,), jnp.int32),
            pltpu.VMEM((ROWS, STRAINS * SLICES, CELLS), jnp.float32),
            pltpu.VMEM((STRAINS * SLICES, PLANE), jnp.float32),
            pltpu.VMEM((TERMS * SLICES, 3 * SLICES * BANDS), jnp.bfloat16),
            pltpu.VMEM((3 * SLICES * BANDS, 2 * PLANE), jnp.bfloat16),
            pltpu.VMEM((ROWS, SLICES * BANDS, CELLS), jnp.float32),
            pltpu.VMEM((SLICES * BANDS, 2 * PLANE), jnp.float32),
            pltpu.VMEM((TERMS * SLICES, 2 * PLANE), jnp.float32),
            pltpu.VMEM((3 * SLICES, NMOM * PLANE), jnp.bfloat16),
            pltpu.VMEM((SLICES, NMOM * PLANE), jnp.float32),
            pltpu.VMEM((NMOM * ROWS, SLICES, CELLS), jnp.float32),
        ],
        compiler_params=params(),
        name="solve",
    )(strain_ids, slice_hop, cross_hop, deform, table, mine, other, *matrices)
    fields, projected = pl.pallas_call(
        gather_kernel,
        out_shape=(shape(2, 2, BANDS * PROBES, CELLS), shape(NMOM, 2, PROBES, PROBES)),
        in_specs=[vmem()],
        out_specs=(vmem(), vmem()),
        compiler_params=params(),
        name="gather",
    )(exchange(blocks, BACK))
    return fields.reshape(2, 2, 1, BANDS, PROBES, 1, CELLS), projected


def solution(mesh):
    placed = (
        P("cuts", None, None, "tile", None),
        P("cuts", None, None, "tile", None),
        P(None, "tile", None),
        P(),
        P(),
        P(),
        P("cuts", "tile", None, None),
        P(),
    )
    return jax.shard_map(
        on_device,
        mesh=mesh,
        in_specs=placed,
        out_specs=(P(None, None, "cuts", None, None, "tile", None), P()),
        check_vma=False,
    )
```

time: 1930 us -> 64.4 us (0.03); the launches traced: 1910 us -> 64.1 us
  waiting for transfers between devices: 835 us -> 2.66 us
  other arithmetic: 633 us -> 0 us
  local copies, waits for them, and re-layouts: 317 us -> 3.78 us
  matrix products: 24.3 us -> 0 us
    all_gather x5 -> x0, waiting for transfers between devices: 423 us -> none  [prefix_2(): everything = jax.tree.map(lambda part: lax.all_gather(part, axis), array)]
    psum x4 -> x0, waiting for transfers between devices: 412 us -> none  [from_root(): return lax.psum(jnp.where(mine, array, jnp.zeros_like(array)), axis)]
    select_n x261 -> x0, other arithmetic: 330 us -> none  [the longest x256 324 us: hop(): return jax.tree.map(lambda a, b: jnp.where(reached, a, b), new, before)]
    dynamic_slice x128 -> x0, local copies, waits for them, and re-layouts: 169 us -> none  [hop(): new = combine(before, jax.tree.map(lambda part: part[at], everything))]
    sub x268 -> x0, other arithmetic: 157 us -> none  [the longest x267 157 us: complex_times(): former[0] * latter[0] - former[1] * latter[1]]
    while x128 -> x0, other arithmetic: 131 us -> none
    slice x129 -> x0, local copies, waits for them, and re-layouts: 102 us -> none  [the longest x128 101 us: complex_times(): latter[1]]
    psum x1 -> x0, blocking collectives: 66.1 us -> none  [on_device(): projected = lax.psum(projected * scale, ('cuts', 'tile'))]
  transfers between devices with their start and end apart: 12 -> 1, of which waited for: 9 -> 1; matrix products, arithmetic and copies ran while one was open for 2% -> 0% of each run, Pallas kernels for 0% -> 0%
where the time goes in v1:
time: 64.4 us; the launch traced here: 64.1 us
  blocking collectives  48.4 us (75%)
  Pallas kernels  8.09 us (13%)
  local copies, waits for them, and re-layouts  3.78 us (6%)
  waiting for transfers between devices  2.66 us (4%)
  between operations  0.77 us (1%)
    all_to_all x2, blocking collectives, exchange(): wide = lax.all_to_all(wide, ALL, split_axis=0, concat_axis=0, tiled=True)  48.4 us
    pallas_call x1, Pallas kernels, on_device(): pl.pallas_call(main, out_shape=shape(DEVICES * BACK, CELLS), in_specs=[sm...  6.7 us
    unnamed x28, local copies, waits for them, and re-layouts  3.78 us
    ppermute x1, waiting for transfers between devices, on_device(): other = lax.ppermute(mine, 'cuts', [(i, i ^ 1) for i in range(cut_count)])  2.66 us
  transfers between devices with their start and end apart: 1, of which 1 were waited for; matrix products, arithmetic and copies ran while one was open for 0% of the time, Pallas kernels for 0%

profile of v1, /device:TPU:1, one launch (start us, length us, event | category | flops | bytes accessed | tf_op | source)
XLA Modules:
  0.0 64.1 jit_solution(10461901012317512933)
XLA Ops:
  0.6 0.0 copy-start.1
  0.6 0.8 %copy-done.1 = f32[1,8,16,1,128]{4,3,2,1,0:T(1,128)S(1)} copy-done((f32[1,8,16,1,128]{4,3,2,1,0:T(1,128)S(1)}, f32[1,8,16,1,128]{4,3,2,1,0:T(1,128)}, u32[]{:S(2)}) %copy-start.1) | copy-done | bytes 65560
  1.5 0.0 copy-start.2
  1.5 0.8 %copy-done.2 = f32[1,8,16,1,128]{4,3,2,1,0:T(1,128)S(1)} copy-done((f32[1,8,16,1,128]{4,3,2,1,0:T(1,128)S(1)}, f32[1,8,16,1,128]{4,3,2,1,0:T(1,128)}, u32[]{:S(2)}) %copy-start.2) | copy-done | bytes 65560
  2.3 0.0 copy-start.6
  2.3 0.7 %copy-done.6 = f32[1,4,6,32]{3,1,2,0:T(4,128)S(1)} copy-done((f32[1,4,6,32]{3,1,2,0:T(4,128)S(1)}, f32[1,4,6,32]{3,1,2,0:T(4,128)}, u32[]{:S(2)}) %copy-start.6) | copy-done | bytes 3096
  3.0 0.0 copy-start.11
  3.0 0.7 %copy-done.11 = f32[8,1,128]{2,1,0:T(1,128)S(1)} copy-done((f32[8,1,128]{2,1,0:T(1,128)S(1)}, f32[8,1,128]{2,1,0:T(1,128)}, u32[]{:S(2)}) %copy-start.11) | copy-done | bytes 4120
  3.7 0.0 copy-start.12
  3.7 0.7 %copy-done.12 = s32[16]{0:T(128)S(1)} copy-done((s32[16]{0:T(128)S(1)}, s32[16]{0:T(128)}, u32[]{:S(2)}) %copy-start.12) | copy-done | bytes 88
  4.4 0.7 %pack.1 = f32[2560,128]{1,0:T(8,128)S(1)} custom-call(s32[16]{0:T(128)S(1)} %copy-done.12, f32[128,128]{1,0:T(8,128)S(1)} %bitcast.20, f32[128,128]{1,0:T(8,128)S(1)} %bitcast.21, f32[6,4,32]{2,1,0:T(4,128)S(1)} %bitcast.22, f32[8,128]{1,0:T(8,128)S(1)} %bitcast.23), custom_call_target="tpu_custom_call" | custom-call | tf_op jit(solution)/shard_map/pack/pallas_call | solution.py:352
  5.0 0.0 copy-start
  5.0 0.0 copy-start.3
  5.0 0.0 copy-start.4
  5.1 0.0 copy-start.5
  5.1 0.0 copy-start.7
  5.1 0.0 copy-start.8
  5.1 0.0 copy-start.9
  5.1 0.0 copy-start.10
  5.1 0.0 copy-start.13
  5.1 33.7 %all_to_all.10 = f32[128,5,4,128]{3,2,1,0:T(4,128)S(1)} all-to-all(f32[128,5,4,128]{3,2,1,0:T(4,128)S(1)} %bitcast.17), channel_id=1, replica_groups=mesh['cuts'=32,'tile'=4] {'cuts','tile'}, dimensions={0} | all-to-all | bytes 2621440 | tf_op jit(solution)/shard_map/all_to_all | solution.py:344
  38.8 0.4 collective-permute-start
  39.2 2.7 %collective-permute-done.refs_6_ = f32[2560,128]{1,0:T(8,128)S(1)} collective-permute-done((f32[2560,128]{1,0:T(8,128)S(1)}, f32[2560,128]{1,0:T(8,128)S(1)}, u32[]{:S(2)}, u32[]{:S(2)}) %collective-permute-start) | collective-permute-done | bytes 1310752 | tf_op jit(solution)/shard_map/ppermute | solution.py:367
  41.9 0.0 copy-done
  41.9 0.0 copy-done.3
  41.9 0.0 copy-done.4
  41.9 0.0 copy-done.5
  41.9 0.0 copy-done.7
  41.9 0.0 copy-done.8
  41.9 0.0 copy-done.9
  41.9 0.0 copy-done.10
  42.0 0.0 copy-done.13
  42.0 6.7 %solve.1 = f32[512,128]{1,0:T(8,128)S(1)} custom-call(s32[16]{0:T(128)S(1)} %copy-done.12, f32[8]{0:T(128)S(1)} %copy-done.13, f32[2,8,8]{2,1,0:T(8,128)S(1)} %copy-done.7, f32[6,8,8]{2,1,0:T(8,128)S(1)} %copy-done.4, f32[10,4]{1,0:T(8,128)S(1)} %copy-done.10, f32[2560,128]{1,0:T(8,128)S(1)} %bitcast.16, f32[2560,128]{1,0:T(8,128)S(1)} %collective-permute-done.refs_6_, ...), custom_call_target="tpu_custom_call" | custom-call | tf_op jit(solution)/shard_map/solve/pallas_call | solution.py:374
  48.7 14.7 %all_to_all.11 = f32[128,1,4,128]{3,2,1,0:T(4,128)S(1)} all-to-all(f32[128,1,4,128]{3,2,1,0:T(4,128)S(1)} %bitcast.18), channel_id=1, replica_groups=mesh['cuts'=32,'tile'=4] {'cuts','tile'}, dimensions={0} | all-to-all | bytes 524288 | tf_op jit(solution)/shard_map/all_to_all | solution.py:344
  63.3 0.7 %gather.1 = (f32[2,2,128,128]{3,2,1,0:T(8,128)}, f32[4,2,16,16]{3,2,1,0:T(8,128)}) custom-call(f32[512,128]{1,0:T(8,128)S(1)} %bitcast.19), custom_call_target="tpu_custom_call" | custom-call | tf_op jit(solution)/shard_map/gather/pallas_call | solution.py:395
Async XLA Ops:
  0.6 0.8 %copy-start.1 = (f32[1,8,16,1,128]{4,3,2,1,0:T(1,128)S(1)}, f32[1,8,16,1,128]{4,3,2,1,0:T(1,128)}, u32[]{:S(2)}) copy-start(f32[1,8,16,1,128]{4,3,2,1,0:T(1,128)} %param.14) | copy-start | bytes 196612
  1.5 0.8 %copy-start.2 = (f32[1,8,16,1,128]{4,3,2,1,0:T(1,128)S(1)}, f32[1,8,16,1,128]{4,3,2,1,0:T(1,128)}, u32[]{:S(2)}) copy-start(f32[1,8,16,1,128]{4,3,2,1,0:T(1,128)} %param.15) | copy-start | bytes 196612
  2.3 0.7 %copy-start.6 = (f32[1,4,6,32]{3,1,2,0:T(4,128)S(1)}, f32[1,4,6,32]{3,1,2,0:T(4,128)}, u32[]{:S(2)}) copy-start(f32[1,4,6,32]{3,1,2,0:T(4,128)} %param.20) | copy-start | bytes 9220
  3.0 0.7 %copy-start.11 = (f32[8,1,128]{2,1,0:T(1,128)S(1)}, f32[8,1,128]{2,1,0:T(1,128)}, u32[]{:S(2)}) copy-start(f32[8,1,128]{2,1,0:T(1,128)} %param.16) | copy-start | bytes 12292
  3.7 0.7 %copy-start.12 = (s32[16]{0:T(128)S(1)}, s32[16]{0:T(128)}, u32[]{:S(2)}) copy-start(s32[16]{0:T(128)} %refs_0_.1) | copy-start | bytes 196
  5.0 36.9 %copy-start = (bf16[256,768]{1,0:T(8,128)(2,1)S(1)}, bf16[256,768]{1,0:T(8,128)(2,1)}, u32[]{:S(2)}) copy-start(bf16[256,768]{1,0:T(8,128)(2,1)} %constant.13.clone.refs_7_) | copy-start | bytes 1179652
  5.0 36.9 %copy-start.3 = (f32[32,256]{1,0:T(8,128)S(1)}, f32[32,256]{1,0:T(8,128)}, u32[]{:S(2)}) copy-start(f32[32,256]{1,0:T(8,128)} %constant.14.clone.refs_8_) | copy-start | bytes 98308
  5.0 36.9 %copy-start.4 = (f32[6,8,8]{2,1,0:T(8,128)S(1)}, f32[6,8,8]{2,1,0:T(8,128)}, u32[]{:S(2)}) copy-start(f32[6,8,8]{2,1,0:T(8,128)} %refs_3_.1) | copy-start | bytes 4612
  5.1 36.9 %copy-start.5 = (f32[32,128]{1,0:T(8,128)S(1)}, f32[32,128]{1,0:T(8,128)}, u32[]{:S(2)}) copy-start(f32[32,128]{1,0:T(8,128)} %constant.17.clone.refs_11_) | copy-start | bytes 49156
  5.1 36.8 %copy-start.7 = (f32[2,8,8]{2,1,0:T(8,128)S(1)}, f32[2,8,8]{2,1,0:T(8,128)}, u32[]{:S(2)}) copy-start(f32[2,8,8]{2,1,0:T(8,128)} %refs_2_.1) | copy-start | bytes 1540
  5.1 36.8 %copy-start.8 = (bf16[32,96]{1,0:T(8,128)(2,1)S(1)}, bf16[32,96]{1,0:T(8,128)(2,1)}, u32[]{:S(2)}) copy-start(bf16[32,96]{1,0:T(8,128)(2,1)} %constant.16.clone.refs_10_) | copy-start | bytes 18436
  5.1 36.8 %copy-start.9 = (bf16[32,96]{1,0:T(8,128)(2,1)S(1)}, bf16[32,96]{1,0:T(8,128)(2,1)}, u32[]{:S(2)}) copy-start(bf16[32,96]{1,0:T(8,128)(2,1)} %constant.15.clone.refs_9_) | copy-start | bytes 18436
  5.1 36.8 %copy-start.10 = (f32[10,4]{1,0:T(8,128)S(1)}, f32[10,4]{1,0:T(8,128)}, u32[]{:S(2)}) copy-start(f32[10,4]{1,0:T(8,128)} %constant.12.clone.refs_4_) | copy-start | bytes 484
  5.1 36.8 %copy-start.13 = (f32[8]{0:T(128)S(1)}, f32[8]{0:T(128)}, u32[]{:S(2)}) copy-start(f32[8]{0:T(128)} %refs_1_.1) | copy-start | bytes 100
  38.8 3.1 %collective-permute-start = (f32[2560,128]{1,0:T(8,128)S(1)}, f32[2560,128]{1,0:T(8,128)S(1)}, u32[]{:S(2)}, u32[]{:S(2)}) collective-permute-start(f32[2560,128]{1,0:T(8,128)S(1)} %bitcast.15), channel_id=1, source_target_pairs={{0,4},{4,0},{8,12},{12,8},{16,20},{20,16},{24,28},{28,24},{32,36},... | collective-permute-start | bytes 3932168 | tf_op jit(solution)/shard_map/ppermute | solution.py:367

commit v2 on v1

v2 whole, which is shorter than its diff:
```python
import math

import jax
import jax.numpy as jnp
import numpy as np
from jax import lax
from jax.experimental import pallas as pl
from jax.experimental.pallas import tpu as pltpu
from jax.sharding import PartitionSpec as P

PTS = 8
NMOM = 4
HALF = PTS // 2
ALL = ("cuts", "tile")

BANDS = 8
CELLS = 128
ROWS = 4
SLICES = 32
PROBES = 16
STRAINS = 6
TERMS = STRAINS + 4
PLANE = ROWS * CELLS
DEVICES = SLICES * ROWS
CHUNK = 20
BACK = 3
NSUB = ROWS * ROWS
HIGHEST = lax.Precision.HIGHEST
VMEM_BYTES = 20 * 1024 * 1024


def pack_kernel(
    probes_hbm,
    test_hbm,
    strain_hbm,
    edge_hbm,
    out_ref,
    probes_ref,
    test_ref,
    strain_ref,
    edge_ref,
    done,
):
    pairs = (
        (probes_hbm, probes_ref),
        (test_hbm, test_ref),
        (strain_hbm, strain_ref),
        (edge_hbm, edge_ref),
    )
    copies = [pltpu.make_async_copy(*pair, done.at[i]) for i, pair in enumerate(pairs)]
    for copy in copies:
        copy.start()
    copies[0].wait()
    for probe in range(PROBES):
        column = probes_ref[pl.ds(probe, BANDS, stride=PROBES), :]
        for band in range(BANDS):
            at = (band * PROBES + probe) * CHUNK
            out_ref[at : at + 8, :] = column
    copies[1].wait()
    for probe in range(PROBES):
        for band in range(BANDS):
            at = (band * PROBES + probe) * CHUNK
            first = band * PROBES + 8 * (probe // 4 % 2)
            out_ref[at + 12 : at + 20, :] = test_ref[first : first + 8, :]
    copies[2].wait()
    copies[3].wait()
    piece = lax.axis_index("cuts") % BANDS
    edge = edge_ref[pl.ds(piece, 1), :]
    strain = jnp.concatenate([strain_ref[:, slot, :] for slot in range(ROWS)], axis=1)
    for half in range(2):
        shared = jnp.concatenate([strain[3 * half : 3 * half + 3], edge], axis=0)
        for probe in range(PROBES):
            if probe // 4 % 2 == half:
                for band in range(BANDS):
                    at = (band * PROBES + probe) * CHUNK
                    out_ref[at + 8 : at + 12, :] = shared


def split(value):
    high = value.astype(jnp.bfloat16)
    low = (value - high.astype(jnp.float32)).astype(jnp.bfloat16)
    return high, low


def matmul(left, right):
    return jnp.dot(left, right, preferred_element_type=jnp.float32)


def prepare_kernel(
    hop_ref,
    cross_ref,
    deform_ref,
    mine_ref,
    wave_ref,
    spread_ref,
    cosine_ref,
    weights_ref,
    waves_ref,
    hop_out_ref,
    shift_ref,
    field_ref,
):
    band = lax.axis_index("cuts") // 4

    for s in range(0, SLICES, 2):
        for row in range(ROWS):
            pair = [
                mine_ref[((s + i) * ROWS + row) * CHUNK : ((s + i) * ROWS + row) * CHUNK + 8, :]
                for i in range(2)
            ]
            high, low = split(jnp.concatenate(pair, axis=0))
            lanes = slice(row * CELLS, (row + 1) * CELLS)
            at = s * BANDS
            field_ref[at : at + 16, lanes] = high
            field_ref[256 + at : 272 + at, lanes] = low
            field_ref[512 + at : 528 + at, lanes] = high
    waves = matmul(wave_ref[...], field_ref[...])
    for row in range(ROWS):
        waves_ref[row] = waves[:, row * CELLS : (row + 1) * CELLS]

    source_band = lax.broadcasted_iota(jnp.int32, (1, SLICES * BANDS), 1) % BANDS
    for term in range(TERMS):
        line = jnp.zeros((1, SLICES * BANDS), jnp.float32)
        for src in range(BANDS):
            if term < STRAINS:
                entry = 0.5 * (deform_ref[term, band, src] + deform_ref[term, src, band])
            else:
                axis = (term - STRAINS) // 2
                if (term - STRAINS) % 2 == 0:
                    entry = cross_ref[axis, band, src]
                else:
                    entry = cross_ref[axis, src, band]
            line = jnp.where(source_band == src, entry, line)
        high, low = split(spread_ref[...] * line)
        at = slice(term * SLICES, (term + 1) * SLICES)
        weights_ref[at, 0:256] = high
        weights_ref[at, 256:512] = high
        weights_ref[at, 512:768] = low

    sub = lax.broadcasted_iota(jnp.int32, (BANDS, CELLS), 0)
    hop = jnp.full((BANDS, CELLS), 2.0 * hop_ref[0], jnp.float32)
    for b in range(1, BANDS):
        hop = jnp.where(sub == b, 2.0 * hop_ref[b], hop)
    hop_out_ref[...] = hop
    shift_ref[...] = 2.0 * hop_ref[band] * cosine_ref[...]


def point_scalar(values, j):
    out = jnp.float32(values[0])
    for i in range(1, HALF):
        out = jnp.where(j == i, jnp.float32(values[i]), out)
    return out


def main_kernel(
    scale,
    cosines,
    table,
    ids_ref,
    mine_ref,
    other_ref,
    weights_ref,
    waves_ref,
    hop_ref,
    shift_ref,
    forth_ref,
    back_ref,
    out_ref,
    place_ref,
    slots_ref,
    strain_ref,
    right_ref,
    result_ref,
    source_ref,
    moment_ref,
    final_ref,
):
    half = lax.axis_index("cuts") % 2
    band = lax.axis_index("cuts") // 4
    lane = lax.broadcasted_iota(jnp.int32, (SLICES, CELLS), 1)

    for slot in range(NSUB):
        place_ref[ids_ref[slot]] = slot
    for holder in range(ROWS):
        for comp in range(3):
            rows = pl.ds(holder * CHUNK + 8 + comp, SLICES, stride=ROWS * CHUNK)
            a = mine_ref[rows, :]
            b = other_ref[rows, :]
            slots_ref[holder, comp * SLICES : (comp + 1) * SLICES, :] = jnp.where(half == 0, a, b)
            slots_ref[holder, (comp + 3) * SLICES : (comp + 4) * SLICES, :] = jnp.where(
                half == 0, b, a
            )
    group = lax.broadcasted_iota(jnp.int32, (STRAINS * SLICES, CELLS), 1) // (CELLS // ROWS)
    for row in range(ROWS):
        total = None
        for part in range(ROWS):
            slot = place_ref[row * ROWS + part]
            shift = ((part + ROWS - slot % ROWS) % ROWS) * (CELLS // ROWS)
            rolled = pltpu.roll(slots_ref[slot // ROWS], shift, 1)
            total = rolled if total is None else jnp.where(group == part, rolled, total)
        strain_ref[:, row * CELLS : (row + 1) * CELLS] = total

    moment_ref[...] = jnp.zeros_like(moment_ref)
    hop = hop_ref[...]

    def point(j, _):
        z_re, z_im = point_scalar(table[0], j), point_scalar(table[1], j)
        square = z_im * z_im
        for row in range(ROWS):
            at_re = row * 2 * CELLS
            gap = z_re - mine_ref[pl.ds(row * CHUNK + 11, BANDS, stride=ROWS * CHUNK), :]
            for pair in range(SLICES // 2):
                parts = []
                for wave in (2 * pair, 2 * pair + 1):
                    if parts and cosines[wave] == cosines[wave - 1]:
                        parts.append(parts[0])
                        continue
                    u = gap + hop * cosines[wave]
                    inverse = 1.0 / (u * u + square)
                    parts.append((u * inverse, -z_im * inverse))
                rows = slice(pair * 16, pair * 16 + 16)
                value = waves_ref[row, rows, :]
                for part in range(2):
                    factor = jnp.concatenate([parts[0][part], parts[1][part]], axis=0)
                    high, low = split(factor * value)
                    lanes = slice(at_re + part * CELLS, at_re + (part + 1) * CELLS)
                    right_ref[rows, lanes] = high
                    right_ref[pair * 16 + 256 : pair * 16 + 272, lanes] = low
                    right_ref[pair * 16 + 512 : pair * 16 + 528, lanes] = high
            lanes = slice(at_re, at_re + 2 * CELLS)
            result_ref[:, lanes] = matmul(weights_ref[...], right_ref[:, lanes])

        for row in range(ROWS):
            for part in range(2):
                at = (2 * row + part) * CELLS
                lanes = slice(at, at + CELLS)
                total = None
                for comp in range(STRAINS):
                    rows = slice(comp * SLICES, (comp + 1) * SLICES)
                    value = strain_ref[rows, row * CELLS : (row + 1) * CELLS] * result_ref[
                        rows, lanes
                    ]
                    total = value if total is None else total + value
                from_right = pltpu.roll(result_ref[192:224, lanes], CELLS - 1, 1)
                from_left = pltpu.roll(result_ref[224:256, lanes], 1, 1)
                total = total + jnp.where(lane < CELLS - 1, from_right, 0.0)
                total = total + jnp.where(lane > 0, from_left, 0.0)
                if row < ROWS - 1:
                    total = total + result_ref[256:288, at + 2 * CELLS : at + 3 * CELLS]
                if row > 0:
                    total = total + result_ref[288:320, at - 2 * CELLS : at - CELLS]
                high, low = split(total)
                source_ref[0:32, lanes] = high
                source_ref[32:64, lanes] = low
                source_ref[64:96, lanes] = high
        result_ref[0:32, :] = matmul(forth_ref[...], source_ref[:, 0 : 2 * PLANE])

        for row in range(ROWS):
            at = row * 2 * CELLS
            edge = mine_ref[pl.ds((band * ROWS + row) * CHUNK + 11, 1), :]
            u = (z_re - edge) + shift_ref[...]
            inverse = 1.0 / (u * u + square)
            g_re = u * inverse
            g_im = -z_im * inverse
            a_re = result_ref[0:32, at : at + CELLS]
            a_re = a_re + waves_ref[row, pl.ds(band, SLICES, stride=BANDS), :]
            a_im = result_ref[0:32, at + CELLS : at + 2 * CELLS]
            v_re = g_re * a_re - g_im * a_im
            v_im = g_re * a_im + g_im * a_re
            for order in range(NMOM):
                lanes = slice(order * PLANE + row * CELLS, order * PLANE + (row + 1) * CELLS)
                w_re = point_scalar(table[2 + order], j)
                w_im = point_scalar(table[2 + NMOM + order], j)
                moment_ref[:, lanes] += w_re * v_re - w_im * v_im
        return 0

    lax.fori_loop(0, HALF, point, 0)

    high, low = split(moment_ref[...])
    source_ref[0:32, :] = high
    source_ref[32:64, :] = low
    source_ref[64:96, :] = high
    final = matmul(back_ref[...], source_ref[...])
    for order in range(NMOM):
        for row in range(ROWS):
            at = order * PLANE + row * CELLS
            value = final[:, at : at + CELLS]
            final_ref[order * ROWS + row] = value
            if order < 2:
                out_ref[pl.ds(row * BACK + order, SLICES, stride=ROWS * BACK), :] = value

    zero = jnp.zeros((8, CELLS), jnp.float32)
    near = [zero] * NMOM
    far = [zero] * NMOM
    for s in range(SLICES):
        for row in range(ROWS):
            at = (s * ROWS + row) * CHUNK + 12
            test_near = mine_ref[at : at + 8, :]
            test_far = other_ref[at : at + 8, :]
            for order in range(NMOM):
                value = final_ref[order * ROWS + row, s : s + 1, :]
                near[order] = near[order] + test_near * value
                far[order] = far[order] + test_far * value
    stack = []
    for order in range(NMOM):
        stack.append(jnp.where(half == 0, near[order], far[order]))
        stack.append(jnp.where(half == 0, far[order], near[order]))
    sums = lax.dot_general(
        jnp.full((8, CELLS), scale, jnp.float32),
        jnp.concatenate(stack, axis=0),
        (((1,), (1,)), ((), ())),
        precision=HIGHEST,
        preferred_element_type=jnp.float32,
    )
    line = jnp.concatenate([sums, jnp.zeros_like(sums)], axis=1)[0:1]
    out_ref[pl.ds(2, DEVICES, stride=BACK), :] = jnp.broadcast_to(line, (DEVICES, CELLS))


def gather_kernel(blocks_ref, fields_ref, projected_ref):
    total = None
    for band in range(BANDS):
        first = band * PROBES * BACK
        for order in range(2):
            fields_ref[order, 0, band * PROBES : (band + 1) * PROBES, :] = blocks_ref[
                pl.ds(first + order, PROBES, stride=BACK), :
            ]
        part = blocks_ref[pl.ds(first + 2, PROBES, stride=BACK), :]
        total = part if total is None else total + part
    turned = total.T
    for order in range(2):
        fields_ref[order, 1] = jnp.zeros((BANDS * PROBES, CELLS), jnp.float32)
    for order in range(NMOM):
        projected_ref[order, 0] = turned[order * PROBES : (order + 1) * PROBES, :]
        projected_ref[order, 1] = jnp.zeros((PROBES, PROBES), jnp.float32)


FREQS = (0, SLICES // 2) + tuple(f for f in range(1, SLICES // 2) for _ in range(2))


def transform():
    s = np.arange(SLICES)
    rows = [np.cos(2 * np.pi * freq * s / SLICES) / np.sqrt(SLICES) for freq in FREQS[:2]]
    for freq in FREQS[2::2]:
        rows.append(np.sqrt(2.0 / SLICES) * np.cos(2 * np.pi * freq * s / SLICES))
        rows.append(np.sqrt(2.0 / SLICES) * np.sin(2 * np.pi * freq * s / SLICES))
    return np.array(rows)


def split_constant(matrix):
    matrix = matrix.astype(np.float32)
    high = matrix.astype(jnp.bfloat16)
    low = (matrix - high.astype(np.float32)).astype(jnp.bfloat16)
    return jnp.asarray(np.concatenate([high, high, low], axis=1))


def constants():
    wave = transform()
    cosine = np.array([math.cos(2 * math.pi * freq / SLICES) for freq in FREQS])
    spread = np.repeat(wave.T, BANDS, axis=1)
    return (
        [float(c) for c in cosine],
        split_constant(np.kron(wave, np.eye(BANDS))),
        jnp.asarray(spread, jnp.float32),
        jnp.asarray(np.repeat(cosine[:, None], CELLS, axis=1), jnp.float32),
        split_constant(wave),
        split_constant(wave.T),
    )


def contour():
    angles = [math.pi * (2 * point + 1) / PTS for point in range(HALF)]
    table = [[math.cos(a) for a in angles], [math.sin(a) for a in angles]]
    for function in (math.cos, math.sin):
        for order in range(NMOM):
            table.append([2.0 / PTS * function((order + 1) * a) for a in angles])
    return table


def vmem():
    return pl.BlockSpec(memory_space=pltpu.VMEM)


def smem():
    return pl.BlockSpec(memory_space=pltpu.SMEM)


def shape(*dims):
    return jax.ShapeDtypeStruct(dims, jnp.float32)


def params():
    return pltpu.CompilerParams(vmem_limit_bytes=VMEM_BYTES)


def exchange(blocks, rows, group):
    wide = blocks.reshape(DEVICES * rows // group, group, CELLS)
    if group > 1:
        wide = wide.reshape(DEVICES, rows // group, group, CELLS)
    wide = lax.all_to_all(wide, ALL, split_axis=0, concat_axis=0, tiled=True)
    return wide.reshape(DEVICES * rows, CELLS)


def on_device(
    probes, test_block, band_edge, slice_hop, cross_hop, deform, strain_elastic, strain_ids
):
    cut_count = lax.axis_size("cuts")
    raw = pl.BlockSpec(memory_space=pltpu.HBM)
    far = lambda x: pltpu.with_memory_space_constraint(x, pltpu.HBM)
    outgoing = pl.pallas_call(
        pack_kernel,
        out_shape=shape(DEVICES * CHUNK, CELLS),
        in_specs=[raw] * 4,
        out_specs=vmem(),
        scratch_shapes=[
            pltpu.VMEM((BANDS * PROBES, CELLS), jnp.float32),
            pltpu.VMEM((BANDS * PROBES, CELLS), jnp.float32),
            pltpu.VMEM((STRAINS, ROWS, CELLS // ROWS), jnp.float32),
            pltpu.VMEM((BANDS, CELLS), jnp.float32),
            pltpu.SemaphoreType.DMA((4,)),
        ],
        compiler_params=params(),
        name="pack",
    )(
        far(probes.reshape(BANDS * PROBES, CELLS)),
        far(test_block.reshape(BANDS * PROBES, CELLS)),
        far(jnp.transpose(strain_elastic[0], (1, 0, 2))),
        far(band_edge.reshape(BANDS, CELLS)),
    )
    mine = exchange(outgoing, CHUNK, 4)
    other = lax.ppermute(mine, "cuts", [(i, i ^ 1) for i in range(cut_count)])
    scale = (cut_count * BANDS * ROWS * CELLS) ** (-0.5)
    cosines, wave, spread, cosine, forth, back = constants()
    table = contour()
    high = lambda *dims: jax.ShapeDtypeStruct(dims, jnp.bfloat16)
    prepared = pl.pallas_call(
        prepare_kernel,
        out_shape=(
            high(TERMS * SLICES, 3 * SLICES * BANDS),
            shape(ROWS, SLICES * BANDS, CELLS),
            shape(BANDS, CELLS),
            shape(SLICES, CELLS),
        ),
        in_specs=[smem()] * 3 + [vmem()] * 4,
        out_specs=(vmem(),) * 4,
        scratch_shapes=[pltpu.VMEM((3 * SLICES * BANDS, PLANE), jnp.bfloat16)],
        compiler_params=params(),
        name="prepare",
    )(slice_hop, cross_hop, deform, mine, wave, spread, cosine)

    def main(*refs):
        main_kernel(scale, cosines, table, *refs)

    blocks = pl.pallas_call(
        main,
        out_shape=shape(DEVICES * BACK, CELLS),
        in_specs=[smem()] + [vmem()] * 8,
        out_specs=vmem(),
        scratch_shapes=[
            pltpu.SMEM((NSUB,), jnp.int32),
            pltpu.VMEM((ROWS, STRAINS * SLICES, CELLS), jnp.float32),
            pltpu.VMEM((STRAINS * SLICES, PLANE), jnp.float32),
            pltpu.VMEM((3 * SLICES * BANDS, 2 * PLANE), jnp.bfloat16),
            pltpu.VMEM((TERMS * SLICES, 2 * PLANE), jnp.float32),
            pltpu.VMEM((3 * SLICES, NMOM * PLANE), jnp.bfloat16),
            pltpu.VMEM((SLICES, NMOM * PLANE), jnp.float32),
            pltpu.VMEM((NMOM * ROWS, SLICES, CELLS), jnp.float32),
        ],
        compiler_params=params(),
        name="solve",
    )(strain_ids, mine, other, *prepared, forth, back)
    fields, projected = pl.pallas_call(
        gather_kernel,
        out_shape=(shape(2, 2, BANDS * PROBES, CELLS), shape(NMOM, 2, PROBES, PROBES)),
        in_specs=[vmem()],
        out_specs=(vmem(), vmem()),
        compiler_params=params(),
        name="gather",
    )(exchange(blocks, BACK, 1))
    return fields.reshape(2, 2, 1, BANDS, PROBES, 1, CELLS), projected


def solution(mesh):
    placed = (
        P("cuts", None, None, "tile", None),
        P("cuts", None, None, "tile", None),
        P(None, "tile", None),
        P(),
        P(),
        P(),
        P("cuts", "tile", None, None),
        P(),
    )
    return jax.shard_map(
        on_device,
        mesh=mesh,
        in_specs=placed,
        out_specs=(P(None, None, "cuts", None, None, "tile", None), P()),
        check_vma=False,
    )
```

time: 64.4 us -> 59.8 us (0.929)
  local copies, waits for them, and re-layouts: 3.78 us -> 0.05 us
  Pallas kernels: 8.09 us -> 9.73 us
  waiting for transfers between devices: 2.66 us -> 1.04 us
  blocking collectives: 48.4 us -> 47.7 us
    unnamed x28 -> x18, local copies, waits for them, and re-layouts: 3.78 us -> 0.05 us
    ppermute x1, waiting for transfers between devices: 2.66 us -> 1.04 us  [on_device(): other = lax.ppermute(mine, 'cuts', [(i, i ^ 1) for i in range(cut_count)])]
    pallas_call x0 -> x1, Pallas kernels: none -> 1.58 us  [on_device(): pl.pallas_call(prepare_kernel, out_shape=(high(TERMS * SLICES, 3 * SLICES...]
    all_to_all x2, blocking collectives: 48.4 us -> 47.7 us  [exchange(): wide = lax.all_to_all(wide, ALL, split_axis=0, concat_axis=0, tiled=True)]
  transfers between devices with their start and end apart: 1 -> 1, of which waited for: 1 -> 1; matrix products, arithmetic and copies ran while one was open for 0% -> 0% of each run, Pallas kernels for 0% -> 3%
where the time goes in v2:
time: 59.8 us; the launch traced here: 59.6 us
  blocking collectives  47.7 us (80%)
  Pallas kernels  9.73 us (16%)
  waiting for transfers between devices  1.04 us (2%)
  between operations  0.72 us (1%)
    all_to_all x2, blocking collectives, exchange(): wide = lax.all_to_all(wide, ALL, split_axis=0, concat_axis=0, tiled=True)  47.7 us
    pallas_call x1, Pallas kernels, on_device(): pl.pallas_call(main, out_shape=shape(DEVICES * BACK, CELLS), in_specs=[sm...  6.34 us
    pallas_call x1, Pallas kernels, on_device(): pl.pallas_call(prepare_kernel, out_shape=(high(TERMS * SLICES, 3 * SLICES...  1.58 us
  transfers between devices with their start and end apart: 1, of which 1 were waited for; matrix products, arithmetic and copies ran while one was open for 0% of the time, Pallas kernels for 3%

profile of v2, /device:TPU:1, one launch (start us, length us, event | category | flops | bytes accessed | tf_op | source)
XLA Modules:
  0.0 59.6 jit_solution(162248419831930588)
XLA Ops:
  0.6 1.1 %pack.1 = f32[2560,128]{1,0:T(8,128)S(1)} custom-call(f32[128,128]{1,0:T(8,128)} %bitcast.21, f32[128,128]{1,0:T(8,128)} %bitcast.22, f32[6,4,32]{2,1,0:T(4,128)} %bitcast.23, f32[8,128]{1,0:T(8,128)} %bitcast.24), custom_call_target="tpu_custom_call" | custom-call | tf_op jit(solution)/shard_map/pack/pallas_call | solution.py:409
  1.7 0.0 copy-start
  1.7 0.0 copy-start.1
  1.7 0.0 copy-start.2
  1.7 0.0 copy-start.3
  1.8 0.0 copy-start.4
  1.8 0.0 copy-start.8
  1.8 33.7 %all_to_all.10 = f32[128,5,4,128]{3,2,1,0:T(4,128)S(1)} all-to-all(f32[128,5,4,128]{3,2,1,0:T(4,128)S(1)} %bitcast.18), channel_id=1, replica_groups=mesh['cuts'=32,'tile'=4] {'cuts','tile'}, dimensions={0} | all-to-all | bytes 2621440 | tf_op jit(solution)/shard_map/all_to_all | solution.py:399
  35.5 0.0 copy-start.5
  35.5 0.0 copy-start.6
  35.5 0.0 copy-start.7
  35.5 0.4 collective-permute-start
  35.9 0.0 copy-done
  35.9 0.0 copy-done.1
  35.9 0.0 copy-done.2
  35.9 0.0 copy-done.3
  35.9 0.0 copy-done.4
  35.9 0.0 copy-done.8
  35.9 1.6 %prepare.1 = (bf16[320,768]{1,0:T(8,128)(2,1)S(1)}, f32[4,256,128]{2,1,0:T(8,128)S(1)}, f32[8,128]{1,0:T(8,128)S(1)}, f32[32,128]{1,0:T(8,128)S(1)}) custom-call(f32[8]{0:T(128)S(1)} %copy-done.8, f32[2,8,8]{2,1,0:T(8,128)S(1)} %copy-done.4, f32[6,8,8]{2,1,0:T(8,128)S(1)} %copy-done.2, f32[2560,128]{1,0:T(8,128)S(1)} %bitcast.16, ...), custom_call_target="tpu_custom_call" | custom-call | tf_op jit(solution)/shard_map/prepare/pallas_call | solution.py:435
  37.5 1.0 %collective-permute-done.refs_2_ = f32[2560,128]{1,0:T(8,128)S(1)} collective-permute-done((f32[2560,128]{1,0:T(8,128)S(1)}, f32[2560,128]{1,0:T(8,128)S(1)}, u32[]{:S(2)}, u32[]{:S(2)}) %collective-permute-start) | collective-permute-done | bytes 1310752 | tf_op jit(solution)/shard_map/ppermute | solution.py:430
  38.6 0.0 copy-done.5
  38.6 0.0 copy-done.6
  38.6 0.0 copy-done.7
  38.6 6.3 %solve.1 = f32[384,128]{1,0:T(8,128)S(1)} custom-call(s32[16]{0:T(128)S(1)} %copy-done.7, f32[2560,128]{1,0:T(8,128)S(1)} %bitcast.17, f32[2560,128]{1,0:T(8,128)S(1)} %collective-permute-done.refs_2_, bf16[320,768]{1,0:T(8,128)(2,1)S(1)} %get-tuple-element.8.refs_3_, f32[4,256,128]{2,1,0:T(8,128)S(1)} %get-tuple-element.9.refs_4_, ...), custom_call_target="tpu_custom_call" | custom-call | tf_op jit(solution)/shard_map/solve/pallas_call | solution.py:453
  44.9 13.9 %all_to_all.11 = f32[384,1,128]{2,1,0:T(1,128)S(1)} all-to-all(f32[384,1,128]{2,1,0:T(1,128)S(1)} %bitcast.19), channel_id=1, replica_groups=mesh['cuts'=32,'tile'=4] {'cuts','tile'}, dimensions={0} | all-to-all | bytes 393216 | tf_op jit(solution)/shard_map/all_to_all | solution.py:399
  58.9 0.7 %gather.1 = (f32[2,2,128,128]{3,2,1,0:T(8,128)}, f32[4,2,16,16]{3,2,1,0:T(8,128)}) custom-call(f32[384,128]{1,0:T(8,128)S(1)} %bitcast.20), custom_call_target="tpu_custom_call" | custom-call | tf_op jit(solution)/shard_map/gather/pallas_call | solution.py:471
Async XLA Ops:
  1.7 34.2 %copy-start = (bf16[256,768]{1,0:T(8,128)(2,1)S(1)}, bf16[256,768]{1,0:T(8,128)(2,1)}, u32[]{:S(2)}) copy-start(bf16[256,768]{1,0:T(8,128)(2,1)} %constant.10.clone.wave_ref) | copy-start | bytes 1179652
  1.7 34.2 %copy-start.1 = (f32[32,256]{1,0:T(8,128)S(1)}, f32[32,256]{1,0:T(8,128)}, u32[]{:S(2)}) copy-start(f32[32,256]{1,0:T(8,128)} %constant.11.clone.spread_ref) | copy-start | bytes 98308
  1.7 34.2 %copy-start.2 = (f32[6,8,8]{2,1,0:T(8,128)S(1)}, f32[6,8,8]{2,1,0:T(8,128)}, u32[]{:S(2)}) copy-start(f32[6,8,8]{2,1,0:T(8,128)} %deform_ref.1) | copy-start | bytes 4612
  1.7 34.2 %copy-start.3 = (f32[32,128]{1,0:T(8,128)S(1)}, f32[32,128]{1,0:T(8,128)}, u32[]{:S(2)}) copy-start(f32[32,128]{1,0:T(8,128)} %constant.12.clone.cosine_ref) | copy-start | bytes 49156
  1.8 34.2 %copy-start.4 = (f32[2,8,8]{2,1,0:T(8,128)S(1)}, f32[2,8,8]{2,1,0:T(8,128)}, u32[]{:S(2)}) copy-start(f32[2,8,8]{2,1,0:T(8,128)} %cross_ref.1) | copy-start | bytes 1540
  1.8 34.2 %copy-start.8 = (f32[8]{0:T(128)S(1)}, f32[8]{0:T(128)}, u32[]{:S(2)}) copy-start(f32[8]{0:T(128)} %hop_ref.1) | copy-start | bytes 100
  35.5 3.1 %copy-start.5 = (bf16[32,96]{1,0:T(8,128)(2,1)S(1)}, bf16[32,96]{1,0:T(8,128)(2,1)}, u32[]{:S(2)}) copy-start(bf16[32,96]{1,0:T(8,128)(2,1)} %constant.14.clone.refs_8_) | copy-start | bytes 18436
  35.5 3.1 %copy-start.6 = (bf16[32,96]{1,0:T(8,128)(2,1)S(1)}, bf16[32,96]{1,0:T(8,128)(2,1)}, u32[]{:S(2)}) copy-start(bf16[32,96]{1,0:T(8,128)(2,1)} %constant.13.clone.refs_7_) | copy-start | bytes 18436
  35.5 3.1 %copy-start.7 = (s32[16]{0:T(128)S(1)}, s32[16]{0:T(128)}, u32[]{:S(2)}) copy-start(s32[16]{0:T(128)} %refs_0_.1) | copy-start | bytes 196
  35.5 3.1 %collective-permute-start = (f32[2560,128]{1,0:T(8,128)S(1)}, f32[2560,128]{1,0:T(8,128)S(1)}, u32[]{:S(2)}, u32[]{:S(2)}) collective-permute-start(f32[2560,128]{1,0:T(8,128)S(1)} %bitcast.15), channel_id=1, source_target_pairs={{0,4},{4,0},{8,12},{12,8},{16,20},{20,16},{24,28},{28,24},{32,36},... | collective-permute-start | bytes 3932168 | tf_op jit(solution)/shard_map/ppermute | solution.py:430

commit v3 on v2

--- a/solution.py
+++ b/solution.py
@@ -27,6 +27,7 @@
 NSUB = ROWS * ROWS
 HIGHEST = lax.Precision.HIGHEST
 VMEM_BYTES = 20 * 1024 * 1024
+PASSES = 1
 
 
 def pack_kernel(
@@ -86,7 +87,21 @@
     return jnp.dot(left, right, preferred_element_type=jnp.float32)
 
 
+def keep(ref, at, lanes, value):
+    size = ref.shape[0] // PASSES
+    rows = slice(at, at + value.shape[0])
+    if PASSES == 1:
+        ref[rows, lanes] = value.astype(jnp.bfloat16)
+        return
+    high, low = split(value)
+    ref[rows, lanes] = high
+    ref[at + size : at + size + value.shape[0], lanes] = low
+    if PASSES == 3:
+        ref[at + 2 * size : at + 2 * size + value.shape[0], lanes] = high
+
+
 def prepare_kernel(
+    cosines,
     hop_ref,
     cross_ref,
     deform_ref,
@@ -94,11 +109,15 @@
     wave_ref,
     spread_ref,
     cosine_ref,
+    result_ref,
+    own_ref,
+    shift_ref,
+    field_ref,
     weights_ref,
     waves_ref,
-    hop_out_ref,
-    shift_ref,
-    field_ref,
+    right_ref,
+    power_ref,
+    value_ref,
 ):
     band = lax.axis_index("cuts") // 4
 
@@ -117,6 +136,9 @@
     waves = matmul(wave_ref[...], field_ref[...])
     for row in range(ROWS):
         waves_ref[row] = waves[:, row * CELLS : (row + 1) * CELLS]
+        own_ref[:, row * CELLS : (row + 1) * CELLS] = waves_ref[
+            row, pl.ds(band, SLICES, stride=BANDS), :
+        ]
 
     source_band = lax.broadcasted_iota(jnp.int32, (1, SLICES * BANDS), 1) % BANDS
     for term in range(TERMS):
@@ -133,35 +155,58 @@
             line = jnp.where(source_band == src, entry, line)
         high, low = split(spread_ref[...] * line)
         at = slice(term * SLICES, (term + 1) * SLICES)
-        weights_ref[at, 0:256] = high
-        weights_ref[at, 256:512] = high
-        weights_ref[at, 512:768] = low
+        for i, part in enumerate((high, high, low)[:PASSES]):
+            weights_ref[at, i * 256 : (i + 1) * 256] = part
 
     sub = lax.broadcasted_iota(jnp.int32, (BANDS, CELLS), 0)
     hop = jnp.full((BANDS, CELLS), 2.0 * hop_ref[0], jnp.float32)
     for b in range(1, BANDS):
         hop = jnp.where(sub == b, 2.0 * hop_ref[b], hop)
-    hop_out_ref[...] = hop
     shift_ref[...] = 2.0 * hop_ref[band] * cosine_ref[...]
 
-
-def point_scalar(values, j):
-    out = jnp.float32(values[0])
-    for i in range(1, HALF):
-        out = jnp.where(j == i, jnp.float32(values[i]), out)
-    return out
+    def fields(row, _):
+        edge = mine_ref[pl.ds(row * CHUNK + 11, BANDS, stride=ROWS * CHUNK), :]
+        for step in range(HALF):
+            for pair in range(SLICES // 2):
+                rows = slice(pair * 16, pair * 16 + 16)
+                if step == 0:
+                    parts = []
+                    for wave in (2 * pair, 2 * pair + 1):
+                        if parts and cosines[wave] == cosines[wave - 1]:
+                            parts.append(parts[0])
+                            continue
+                        energy = edge - hop * cosines[wave]
+                        eighth = energy * energy
+                        eighth = eighth * eighth
+                        eighth = eighth * eighth
+                        parts.append((energy, 1.0 / (1.0 + eighth)))
+                    energy = jnp.concatenate([parts[0][0], parts[1][0]], axis=0)
+                    inverse = jnp.concatenate([parts[0][1], parts[1][1]], axis=0)
+                    value = inverse * waves_ref[row, rows, :]
+                    power_ref[rows, :] = energy
+                else:
+                    energy = power_ref[rows, :]
+                    value = value_ref[rows, :]
+                after = value * energy
+                for part, kept in enumerate((value, after)):
+                    at = (2 * step + part) * CELLS
+                    keep(right_ref, pair * 16, slice(at, at + CELLS), kept)
+                if step < HALF - 1:
+                    value_ref[rows, :] = after * energy
+            lanes = slice(2 * step * CELLS, (2 * step + 2) * CELLS)
+            result_ref[row, :, lanes] = matmul(weights_ref[...], right_ref[:, lanes])
+        return 0
+
+    lax.fori_loop(0, ROWS, fields, 0)
 
 
 def main_kernel(
     scale,
-    cosines,
-    table,
     ids_ref,
     mine_ref,
     other_ref,
-    weights_ref,
-    waves_ref,
-    hop_ref,
+    result_ref,
+    own_ref,
     shift_ref,
     forth_ref,
     back_ref,
@@ -169,8 +214,6 @@
     place_ref,
     slots_ref,
     strain_ref,
-    right_ref,
-    result_ref,
     source_ref,
     moment_ref,
     final_ref,
@@ -200,81 +243,54 @@
             total = rolled if total is None else jnp.where(group == part, rolled, total)
         strain_ref[:, row * CELLS : (row + 1) * CELLS] = total
 
-    moment_ref[...] = jnp.zeros_like(moment_ref)
-    hop = hop_ref[...]
-
-    def point(j, _):
-        z_re, z_im = point_scalar(table[0], j), point_scalar(table[1], j)
-        square = z_im * z_im
-        for row in range(ROWS):
-            at_re = row * 2 * CELLS
-            gap = z_re - mine_ref[pl.ds(row * CHUNK + 11, BANDS, stride=ROWS * CHUNK), :]
-            for pair in range(SLICES // 2):
-                parts = []
-                for wave in (2 * pair, 2 * pair + 1):
-                    if parts and cosines[wave] == cosines[wave - 1]:
-                        parts.append(parts[0])
-                        continue
-                    u = gap + hop * cosines[wave]
-                    inverse = 1.0 / (u * u + square)
-                    parts.append((u * inverse, -z_im * inverse))
-                rows = slice(pair * 16, pair * 16 + 16)
-                value = waves_ref[row, rows, :]
-                for part in range(2):
-                    factor = jnp.concatenate([parts[0][part], parts[1][part]], axis=0)
-                    high, low = split(factor * value)
-                    lanes = slice(at_re + part * CELLS, at_re + (part + 1) * CELLS)
-                    right_ref[rows, lanes] = high
-                    right_ref[pair * 16 + 256 : pair * 16 + 272, lanes] = low
-                    right_ref[pair * 16 + 512 : pair * 16 + 528, lanes] = high
-            lanes = slice(at_re, at_re + 2 * CELLS)
-            result_ref[:, lanes] = matmul(weights_ref[...], right_ref[:, lanes])
-
-        for row in range(ROWS):
-            for part in range(2):
-                at = (2 * row + part) * CELLS
-                lanes = slice(at, at + CELLS)
-                total = None
-                for comp in range(STRAINS):
-                    rows = slice(comp * SLICES, (comp + 1) * SLICES)
-                    value = strain_ref[rows, row * CELLS : (row + 1) * CELLS] * result_ref[
-                        rows, lanes
-                    ]
-                    total = value if total is None else total + value
-                from_right = pltpu.roll(result_ref[192:224, lanes], CELLS - 1, 1)
-                from_left = pltpu.roll(result_ref[224:256, lanes], 1, 1)
-                total = total + jnp.where(lane < CELLS - 1, from_right, 0.0)
-                total = total + jnp.where(lane > 0, from_left, 0.0)
-                if row < ROWS - 1:
-                    total = total + result_ref[256:288, at + 2 * CELLS : at + 3 * CELLS]
-                if row > 0:
-                    total = total + result_ref[288:320, at - 2 * CELLS : at - CELLS]
-                high, low = split(total)
-                source_ref[0:32, lanes] = high
-                source_ref[32:64, lanes] = low
-                source_ref[64:96, lanes] = high
-        result_ref[0:32, :] = matmul(forth_ref[...], source_ref[:, 0 : 2 * PLANE])
-
-        for row in range(ROWS):
-            at = row * 2 * CELLS
-            edge = mine_ref[pl.ds((band * ROWS + row) * CHUNK + 11, 1), :]
-            u = (z_re - edge) + shift_ref[...]
-            inverse = 1.0 / (u * u + square)
-            g_re = u * inverse
-            g_im = -z_im * inverse
-            a_re = result_ref[0:32, at : at + CELLS]
-            a_re = a_re + waves_ref[row, pl.ds(band, SLICES, stride=BANDS), :]
-            a_im = result_ref[0:32, at + CELLS : at + 2 * CELLS]
-            v_re = g_re * a_re - g_im * a_im
-            v_im = g_re * a_im + g_im * a_re
-            for order in range(NMOM):
-                lanes = slice(order * PLANE + row * CELLS, order * PLANE + (row + 1) * CELLS)
-                w_re = point_scalar(table[2 + order], j)
-                w_im = point_scalar(table[2 + NMOM + order], j)
-                moment_ref[:, lanes] += w_re * v_re - w_im * v_im
-        return 0
-
-    lax.fori_loop(0, HALF, point, 0)
+    for row in range(ROWS):
+        strains = [
+            strain_ref[comp * SLICES : (comp + 1) * SLICES, row * CELLS : (row + 1) * CELLS]
+            for comp in range(STRAINS)
+        ]
+        for field in range(PTS):
+            lanes = slice(field * CELLS, (field + 1) * CELLS)
+            total = None
+            for comp in range(STRAINS):
+                rows = slice(comp * SLICES, (comp + 1) * SLICES)
+                value = strains[comp] * result_ref[row, rows, lanes]
+                total = value if total is None else total + value
+            from_right = pltpu.roll(result_ref[row, 192:224, lanes], CELLS - 1, 1)
+            from_left = pltpu.roll(result_ref[row, 224:256, lanes], 1, 1)
+            total = total + jnp.where(lane < CELLS - 1, from_right, 0.0)
+            total = total + jnp.where(lane > 0, from_left, 0.0)
+            if row < ROWS - 1:
+                total = total + result_ref[row + 1, 256:288, lanes]
+            if row > 0:
+                total = total + result_ref[row - 1, 288:320, lanes]
+            high, low = split(total)
+            source_ref[0:32, lanes] = high
+            source_ref[32:64, lanes] = low
+            source_ref[64:96, lanes] = high
+        coupled = matmul(forth_ref[...], source_ref[:, 0 : PTS * CELLS])
+        terms = [coupled[:, field * CELLS : (field + 1) * CELLS] for field in range(PTS)]
+
+        edge = mine_ref[pl.ds((band * ROWS + row) * CHUNK + 11, 1), :]
+        energy = edge - shift_ref[...]
+        powers = [None, energy]
+        for _ in range(2, PTS):
+            powers.append(powers[-1] * energy)
+        inverse = 1.0 / (1.0 + powers[4] * powers[4])
+        own = own_ref[:, row * CELLS : (row + 1) * CELLS]
+        upper = terms[3]
+        for field in range(4, PTS):
+            upper = upper * energy + terms[field]
+        uppers = [None, None, None, upper]
+        for order in (2, 1, 0):
+            uppers[order] = uppers[order + 1] + powers[PTS - 1 - order] * terms[order]
+        lower = None
+        for order in range(NMOM):
+            value = own - uppers[order]
+            if order > 0:
+                lower = terms[0] if order == 1 else lower * energy + terms[order - 1]
+                value = lower + powers[order] * value
+            lanes = slice(order * PLANE + row * CELLS, order * PLANE + (row + 1) * CELLS)
+            moment_ref[:, lanes] = inverse * value
 
     high, low = split(moment_ref[...])
     source_ref[0:32, :] = high
@@ -365,15 +381,6 @@
         split_constant(wave),
         split_constant(wave.T),
     )
-
-
-def contour():
-    angles = [math.pi * (2 * point + 1) / PTS for point in range(HALF)]
-    table = [[math.cos(a) for a in angles], [math.sin(a) for a in angles]]
-    for function in (math.cos, math.sin):
-        for order in range(NMOM):
-            table.append([2.0 / PTS * function((order + 1) * a) for a in angles])
-    return table
 
 
 def vmem():
@@ -430,37 +437,44 @@
     other = lax.ppermute(mine, "cuts", [(i, i ^ 1) for i in range(cut_count)])
     scale = (cut_count * BANDS * ROWS * CELLS) ** (-0.5)
     cosines, wave, spread, cosine, forth, back = constants()
-    table = contour()
-    high = lambda *dims: jax.ShapeDtypeStruct(dims, jnp.bfloat16)
+    wide = SLICES * BANDS
+
+    def prepare(*refs):
+        prepare_kernel(cosines, *refs)
+
     prepared = pl.pallas_call(
-        prepare_kernel,
+        prepare,
         out_shape=(
-            high(TERMS * SLICES, 3 * SLICES * BANDS),
-            shape(ROWS, SLICES * BANDS, CELLS),
-            shape(BANDS, CELLS),
+            shape(ROWS, TERMS * SLICES, PTS * CELLS),
+            shape(SLICES, PLANE),
             shape(SLICES, CELLS),
         ),
         in_specs=[smem()] * 3 + [vmem()] * 4,
-        out_specs=(vmem(),) * 4,
-        scratch_shapes=[pltpu.VMEM((3 * SLICES * BANDS, PLANE), jnp.bfloat16)],
+        out_specs=(vmem(),) * 3,
+        scratch_shapes=[
+            pltpu.VMEM((3 * wide, PLANE), jnp.bfloat16),
+            pltpu.VMEM((TERMS * SLICES, PASSES * wide), jnp.bfloat16),
+            pltpu.VMEM((ROWS, wide, CELLS), jnp.float32),
+            pltpu.VMEM((PASSES * wide, PTS * CELLS), jnp.bfloat16),
+            pltpu.VMEM((wide, CELLS), jnp.float32),
+            pltpu.VMEM((wide, CELLS), jnp.float32),
+        ],
         compiler_params=params(),
         name="prepare",
     )(slice_hop, cross_hop, deform, mine, wave, spread, cosine)
 
     def main(*refs):
-        main_kernel(scale, cosines, table, *refs)
+        main_kernel(scale, *refs)
 
     blocks = pl.pallas_call(
         main,
         out_shape=shape(DEVICES * BACK, CELLS),
-        in_specs=[smem()] + [vmem()] * 8,
+        in_specs=[smem()] + [vmem()] * 7,
         out_specs=vmem(),
         scratch_shapes=[
             pltpu.SMEM((NSUB,), jnp.int32),
             pltpu.VMEM((ROWS, STRAINS * SLICES, CELLS), jnp.float32),
             pltpu.VMEM((STRAINS * SLICES, PLANE), jnp.float32),
-            pltpu.VMEM((3 * SLICES * BANDS, 2 * PLANE), jnp.bfloat16),
-            pltpu.VMEM((TERMS * SLICES, 2 * PLANE), jnp.float32),
             pltpu.VMEM((3 * SLICES, NMOM * PLANE), jnp.bfloat16),
             pltpu.VMEM((SLICES, NMOM * PLANE), jnp.float32),
             pltpu.VMEM((NMOM * ROWS, SLICES, CELLS), jnp.float32),

time: 59.8 us -> 56.3 us (0.941)
  Pallas kernels: 9.73 us -> 7.46 us
  waiting for transfers between devices: 1.04 us -> 0.01 us
    pallas_call x1, Pallas kernels: 6.34 us -> 2.6 us  [on_device(): pl.pallas_call(main, out_shape=shape(DEVICES * BACK, CELLS), in_specs=[sm...]
    pallas_call x1, Pallas kernels: 1.58 us -> 3.06 us  [on_device(): pl.pallas_call(prepare, out_shape=(shape(ROWS, TERMS * SLICES, PTS * CELL...]
    ppermute x1, waiting for transfers between devices: 1.04 us -> 0.01 us  [on_device(): other = lax.ppermute(mine, 'cuts', [(i, i ^ 1) for i in range(cut_count)])]
  transfers between devices with their start and end apart: 1 -> 1, of which waited for: 1 -> 0; matrix products, arithmetic and copies ran while one was open for 0% -> 0% of each run, Pallas kernels for 3% -> 5%
where the time goes in v3:
time: 56.3 us; the launch traced here: 56.1 us
  blocking collectives  47.4 us (84%)
  Pallas kernels  7.46 us (13%)
  between operations  0.75 us (1%)
    all_to_all x2, blocking collectives, exchange(): wide = lax.all_to_all(wide, ALL, split_axis=0, concat_axis=0, tiled=True)  47.4 us
    pallas_call x1, Pallas kernels, on_device(): pl.pallas_call(prepare, out_shape=(shape(ROWS, TERMS * SLICES, PTS * CELL...  3.06 us
    pallas_call x1, Pallas kernels, on_device(): pl.pallas_call(main, out_shape=shape(DEVICES * BACK, CELLS), in_specs=[sm...  2.6 us
  transfers between devices with their start and end apart: 1, of which 0 were waited for; matrix products, arithmetic and copies ran while one was open for 0% of the time, Pallas kernels for 5%

profile of v3, /device:TPU:1, one launch (start us, length us, event | category | flops | bytes accessed | tf_op | source)
XLA Modules:
  0.0 56.1 jit_solution(12615930478103046828)
XLA Ops:
  0.6 1.1 %pack.1 = f32[2560,128]{1,0:T(8,128)S(1)} custom-call(f32[128,128]{1,0:T(8,128)} %bitcast.21, f32[128,128]{1,0:T(8,128)} %bitcast.22, f32[6,4,32]{2,1,0:T(4,128)} %bitcast.23, f32[8,128]{1,0:T(8,128)} %bitcast.24), custom_call_target="tpu_custom_call" | custom-call | tf_op jit(solution)/shard_map/pack/pallas_call | solution.py:416
  1.7 0.0 copy-start
  1.7 0.0 copy-start.1
  1.7 0.0 copy-start.2
  1.7 0.0 copy-start.3
  1.8 0.0 copy-start.4
  1.8 0.0 copy-start.8
  1.8 33.7 %all_to_all.10 = f32[128,5,4,128]{3,2,1,0:T(4,128)S(1)} all-to-all(f32[128,5,4,128]{3,2,1,0:T(4,128)S(1)} %bitcast.18), channel_id=1, replica_groups=mesh['cuts'=32,'tile'=4] {'cuts','tile'}, dimensions={0} | all-to-all | bytes 2621440 | tf_op jit(solution)/shard_map/all_to_all | solution.py:406
  35.5 0.0 copy-start.5
  35.5 0.0 copy-start.6
  35.5 0.0 copy-start.7
  35.5 0.4 collective-permute-start
  35.9 0.0 copy-done
  35.9 0.0 copy-done.1
  35.9 0.0 copy-done.2
  35.9 0.0 copy-done.3
  35.9 0.0 copy-done.4
  35.9 0.0 copy-done.8
  35.9 3.1 %prepare.1 = (f32[4,320,1024]{2,1,0:T(8,128)S(1)}, f32[32,512]{1,0:T(8,128)S(1)}, f32[32,128]{1,0:T(8,128)S(1)}) custom-call(f32[8]{0:T(128)S(1)} %copy-done.8, f32[2,8,8]{2,1,0:T(8,128)S(1)} %copy-done.4, f32[6,8,8]{2,1,0:T(8,128)S(1)} %copy-done.2, f32[2560,128]{1,0:T(8,128)S(1)} %bitcast.16, bf16[256,768]{1,0:T(8,128)(2,1)S(1)} %copy-done, ...), custom_call_target="tpu_custom_call" | custom-call | tf_op jit(solution)/shard_map/prepare/pallas_call | solution.py:445
  39.0 0.0 collective-permute-done.refs_2_
  39.0 0.0 copy-done.5
  39.0 0.0 copy-done.6
  39.0 0.0 copy-done.7
  39.0 2.6 %solve.1 = f32[384,128]{1,0:T(8,128)S(1)} custom-call(s32[16]{0:T(128)S(1)} %copy-done.7, f32[2560,128]{1,0:T(8,128)S(1)} %bitcast.17, f32[2560,128]{1,0:T(8,128)S(1)} %collective-permute-done.refs_2_, f32[4,320,1024]{2,1,0:T(8,128)S(1)} %get-tuple-element.7.refs_3_, f32[32,512]{1,0:T(8,128)S(1)} %get-tuple-element.8.refs_4_, ...), custom_call_target="tpu_custom_call" | custom-call | tf_op jit(solution)/shard_map/solve/pallas_call | solution.py:469
  41.6 13.7 %all_to_all.11 = f32[384,1,128]{2,1,0:T(1,128)S(1)} all-to-all(f32[384,1,128]{2,1,0:T(1,128)S(1)} %bitcast.20), channel_id=1, replica_groups=mesh['cuts'=32,'tile'=4] {'cuts','tile'}, dimensions={0} | all-to-all | bytes 393216 | tf_op jit(solution)/shard_map/all_to_all | solution.py:406
  55.3 0.7 %gather.1 = (f32[2,2,128,128]{3,2,1,0:T(8,128)}, f32[4,2,16,16]{3,2,1,0:T(8,128)}) custom-call(f32[384,128]{1,0:T(8,128)S(1)} %bitcast.19), custom_call_target="tpu_custom_call" | custom-call | tf_op jit(solution)/shard_map/gather/pallas_call | solution.py:485
Async XLA Ops:
  1.7 34.2 %copy-start = (bf16[256,768]{1,0:T(8,128)(2,1)S(1)}, bf16[256,768]{1,0:T(8,128)(2,1)}, u32[]{:S(2)}) copy-start(bf16[256,768]{1,0:T(8,128)(2,1)} %constant.10.clone.refs_4_) | copy-start | bytes 1179652
  1.7 34.2 %copy-start.1 = (f32[32,256]{1,0:T(8,128)S(1)}, f32[32,256]{1,0:T(8,128)}, u32[]{:S(2)}) copy-start(f32[32,256]{1,0:T(8,128)} %constant.11.clone.refs_5_) | copy-start | bytes 98308
  1.7 34.2 %copy-start.2 = (f32[6,8,8]{2,1,0:T(8,128)S(1)}, f32[6,8,8]{2,1,0:T(8,128)}, u32[]{:S(2)}) copy-start(f32[6,8,8]{2,1,0:T(8,128)} %refs_2_.1) | copy-start | bytes 4612
  1.7 34.2 %copy-start.3 = (f32[32,128]{1,0:T(8,128)S(1)}, f32[32,128]{1,0:T(8,128)}, u32[]{:S(2)}) copy-start(f32[32,128]{1,0:T(8,128)} %constant.12.clone.refs_6_) | copy-start | bytes 49156
  1.8 34.2 %copy-start.4 = (f32[2,8,8]{2,1,0:T(8,128)S(1)}, f32[2,8,8]{2,1,0:T(8,128)}, u32[]{:S(2)}) copy-start(f32[2,8,8]{2,1,0:T(8,128)} %refs_1_.1) | copy-start | bytes 1540
  1.8 34.2 %copy-start.8 = (f32[8]{0:T(128)S(1)}, f32[8]{0:T(128)}, u32[]{:S(2)}) copy-start(f32[8]{0:T(128)} %refs_0_.2) | copy-start | bytes 100
  35.5 3.5 %copy-start.5 = (bf16[32,96]{1,0:T(8,128)(2,1)S(1)}, bf16[32,96]{1,0:T(8,128)(2,1)}, u32[]{:S(2)}) copy-start(bf16[32,96]{1,0:T(8,128)(2,1)} %constant.14.clone.refs_7_) | copy-start | bytes 18436
  35.5 3.5 %copy-start.6 = (bf16[32,96]{1,0:T(8,128)(2,1)S(1)}, bf16[32,96]{1,0:T(8,128)(2,1)}, u32[]{:S(2)}) copy-start(bf16[32,96]{1,0:T(8,128)(2,1)} %constant.13.clone.refs_6_) | copy-start | bytes 18436
  35.5 3.5 %copy-start.7 = (s32[16]{0:T(128)S(1)}, s32[16]{0:T(128)}, u32[]{:S(2)}) copy-start(s32[16]{0:T(128)} %refs_0_.3) | copy-start | bytes 196
  35.5 3.5 %collective-permute-start = (f32[2560,128]{1,0:T(8,128)S(1)}, f32[2560,128]{1,0:T(8,128)S(1)}, u32[]{:S(2)}, u32[]{:S(2)}) collective-permute-start(f32[2560,128]{1,0:T(8,128)S(1)} %bitcast.15), channel_id=1, source_target_pairs={{0,4},{4,0},{8,12},{12,8},{16,20},{20,16},{24,28},{28,24},{32,36},... | collective-permute-start | bytes 3932168 | tf_op jit(solution)/shard_map/ppermute | solution.py:437

commit v4 on v3

--- a/solution.py
+++ b/solution.py
@@ -102,24 +102,42 @@
 
 def prepare_kernel(
     cosines,
-    hop_ref,
-    cross_ref,
-    deform_ref,
+    hop_hbm,
+    cross_hbm,
+    deform_hbm,
+    ids_hbm,
     mine_ref,
     wave_ref,
     spread_ref,
     cosine_ref,
     result_ref,
+    hops_ref,
     own_ref,
     shift_ref,
+    place_ref,
+    hop_ref,
+    cross_ref,
+    deform_ref,
+    ids_ref,
+    done,
     field_ref,
     weights_ref,
     waves_ref,
     right_ref,
     power_ref,
     value_ref,
+    across_ref,
 ):
     band = lax.axis_index("cuts") // 4
+    pairs = (
+        (hop_hbm, hop_ref),
+        (cross_hbm, cross_ref),
+        (deform_hbm, deform_ref),
+        (ids_hbm, ids_ref),
+    )
+    copies = [pltpu.make_async_copy(*pair, done.at[i]) for i, pair in enumerate(pairs)]
+    for copy in copies:
+        copy.start()
 
     for s in range(0, SLICES, 2):
         for row in range(ROWS):
@@ -140,6 +158,17 @@
             row, pl.ds(band, SLICES, stride=BANDS), :
         ]
 
+    for copy in copies:
+        copy.wait()
+
+    width = CELLS // ROWS
+    slot_cell = lax.broadcasted_iota(jnp.int32, (width, PLANE), 0)
+    cell = lax.broadcasted_iota(jnp.int32, (width, PLANE), 1)
+    diagonal = jnp.where(cell % width == slot_cell, cell // width, -1)
+    for slot in range(NSUB):
+        match = jnp.where(diagonal == ids_ref[slot], 1.0, 0.0)
+        place_ref[slot * width : (slot + 1) * width, :] = match.astype(jnp.bfloat16)
+
     source_band = lax.broadcasted_iota(jnp.int32, (1, SLICES * BANDS), 1) % BANDS
     for term in range(TERMS):
         line = jnp.zeros((1, SLICES * BANDS), jnp.float32)
@@ -163,6 +192,8 @@
     for b in range(1, BANDS):
         hop = jnp.where(sub == b, 2.0 * hop_ref[b], hop)
     shift_ref[...] = 2.0 * hop_ref[band] * cosine_ref[...]
+
+    lane = lax.broadcasted_iota(jnp.int32, (SLICES, CELLS), 1)
 
     def fields(row, _):
         edge = mine_ref[pl.ds(row * CHUNK + 11, BANDS, stride=ROWS * CHUNK), :]
@@ -194,25 +225,42 @@
                 if step < HALF - 1:
                     value_ref[rows, :] = after * energy
             lanes = slice(2 * step * CELLS, (2 * step + 2) * CELLS)
-            result_ref[row, :, lanes] = matmul(weights_ref[...], right_ref[:, lanes])
+            product = matmul(weights_ref[...], right_ref[:, lanes])
+            result_ref[row, :, lanes] = product[0:192]
+            across_ref[row, :, lanes] = product[256:320]
+            for part in range(2):
+                own = slice(part * CELLS, (part + 1) * CELLS)
+                from_right = pltpu.roll(product[192:224, own], CELLS - 1, 1)
+                from_left = pltpu.roll(product[224:256, own], 1, 1)
+                at = (2 * step + part) * CELLS
+                hops_ref[row, :, at : at + CELLS] = jnp.where(
+                    lane < CELLS - 1, from_right, 0.0
+                ) + jnp.where(lane > 0, from_left, 0.0)
         return 0
 
-    lax.fori_loop(0, ROWS, fields, 0)
+    for row in range(ROWS):
+        fields(row, 0)
+    for row in range(ROWS):
+        if row < ROWS - 1:
+            hops_ref[row] += across_ref[row + 1, 0:32]
+        if row > 0:
+            hops_ref[row] += across_ref[row - 1, 32:64]
 
 
 def main_kernel(
     scale,
-    ids_ref,
     mine_ref,
     other_ref,
     result_ref,
+    hops_ref,
     own_ref,
     shift_ref,
+    place_ref,
     forth_ref,
     back_ref,
     out_ref,
-    place_ref,
-    slots_ref,
+    high_ref,
+    low_ref,
     strain_ref,
     source_ref,
     moment_ref,
@@ -220,28 +268,18 @@
 ):
     half = lax.axis_index("cuts") % 2
     band = lax.axis_index("cuts") // 4
-    lane = lax.broadcasted_iota(jnp.int32, (SLICES, CELLS), 1)
-
-    for slot in range(NSUB):
-        place_ref[ids_ref[slot]] = slot
+
     for holder in range(ROWS):
+        lanes = slice(holder * CELLS, (holder + 1) * CELLS)
         for comp in range(3):
             rows = pl.ds(holder * CHUNK + 8 + comp, SLICES, stride=ROWS * CHUNK)
             a = mine_ref[rows, :]
             b = other_ref[rows, :]
-            slots_ref[holder, comp * SLICES : (comp + 1) * SLICES, :] = jnp.where(half == 0, a, b)
-            slots_ref[holder, (comp + 3) * SLICES : (comp + 4) * SLICES, :] = jnp.where(
-                half == 0, b, a
-            )
-    group = lax.broadcasted_iota(jnp.int32, (STRAINS * SLICES, CELLS), 1) // (CELLS // ROWS)
-    for row in range(ROWS):
-        total = None
-        for part in range(ROWS):
-            slot = place_ref[row * ROWS + part]
-            shift = ((part + ROWS - slot % ROWS) % ROWS) * (CELLS // ROWS)
-            rolled = pltpu.roll(slots_ref[slot // ROWS], shift, 1)
-            total = rolled if total is None else jnp.where(group == part, rolled, total)
-        strain_ref[:, row * CELLS : (row + 1) * CELLS] = total
+            for at, value in ((comp, jnp.where(half == 0, a, b)), (comp + 3, jnp.where(half == 0, b, a))):
+                high, low = split(value)
+                high_ref[at * SLICES : (at + 1) * SLICES, lanes] = high
+                low_ref[at * SLICES : (at + 1) * SLICES, lanes] = low
+    strain_ref[...] = matmul(high_ref[...], place_ref[...]) + matmul(low_ref[...], place_ref[...])
 
     for row in range(ROWS):
         strains = [
@@ -250,19 +288,10 @@
         ]
         for field in range(PTS):
             lanes = slice(field * CELLS, (field + 1) * CELLS)
-            total = None
+            total = hops_ref[row, :, lanes]
             for comp in range(STRAINS):
                 rows = slice(comp * SLICES, (comp + 1) * SLICES)
-                value = strains[comp] * result_ref[row, rows, lanes]
-                total = value if total is None else total + value
-            from_right = pltpu.roll(result_ref[row, 192:224, lanes], CELLS - 1, 1)
-            from_left = pltpu.roll(result_ref[row, 224:256, lanes], 1, 1)
-            total = total + jnp.where(lane < CELLS - 1, from_right, 0.0)
-            total = total + jnp.where(lane > 0, from_left, 0.0)
-            if row < ROWS - 1:
-                total = total + result_ref[row + 1, 256:288, lanes]
-            if row > 0:
-                total = total + result_ref[row - 1, 288:320, lanes]
+                total = total + strains[comp] * result_ref[row, rows, lanes]
             high, low = split(total)
             source_ref[0:32, lanes] = high
             source_ref[32:64, lanes] = low
@@ -385,10 +414,6 @@
 
 def vmem():
     return pl.BlockSpec(memory_space=pltpu.VMEM)
-
-
-def smem():
-    return pl.BlockSpec(memory_space=pltpu.SMEM)
 
 
 def shape(*dims):
@@ -445,23 +470,31 @@
     prepared = pl.pallas_call(
         prepare,
         out_shape=(
-            shape(ROWS, TERMS * SLICES, PTS * CELLS),
+            shape(ROWS, STRAINS * SLICES, PTS * CELLS),
+            shape(ROWS, SLICES, PTS * CELLS),
             shape(SLICES, PLANE),
             shape(SLICES, CELLS),
+            jax.ShapeDtypeStruct((PLANE, PLANE), jnp.bfloat16),
         ),
-        in_specs=[smem()] * 3 + [vmem()] * 4,
-        out_specs=(vmem(),) * 3,
+        in_specs=[raw] * 4 + [vmem()] * 4,
+        out_specs=(vmem(),) * 5,
         scratch_shapes=[
+            pltpu.SMEM(slice_hop.shape, jnp.float32),
+            pltpu.SMEM(cross_hop.shape, jnp.float32),
+            pltpu.SMEM(deform.shape, jnp.float32),
+            pltpu.SMEM(strain_ids.shape, jnp.int32),
+            pltpu.SemaphoreType.DMA((4,)),
             pltpu.VMEM((3 * wide, PLANE), jnp.bfloat16),
             pltpu.VMEM((TERMS * SLICES, PASSES * wide), jnp.bfloat16),
             pltpu.VMEM((ROWS, wide, CELLS), jnp.float32),
             pltpu.VMEM((PASSES * wide, PTS * CELLS), jnp.bfloat16),
             pltpu.VMEM((wide, CELLS), jnp.float32),
             pltpu.VMEM((wide, CELLS), jnp.float32),
+            pltpu.VMEM((ROWS, 2 * SLICES, PTS * CELLS), jnp.float32),
         ],
         compiler_params=params(),
         name="prepare",
-    )(slice_hop, cross_hop, deform, mine, wave, spread, cosine)
+    )(*map(far, (slice_hop, cross_hop, deform, strain_ids)), mine, wave, spread, cosine)
 
     def main(*refs):
         main_kernel(scale, *refs)
@@ -469,11 +502,11 @@
     blocks = pl.pallas_call(
         main,
         out_shape=shape(DEVICES * BACK, CELLS),
-        in_specs=[smem()] + [vmem()] * 7,
+        in_specs=[vmem()] * 9,
         out_specs=vmem(),
         scratch_shapes=[
-            pltpu.SMEM((NSUB,), jnp.int32),
-            pltpu.VMEM((ROWS, STRAINS * SLICES, CELLS), jnp.float32),
+            pltpu.VMEM((STRAINS * SLICES, PLANE), jnp.bfloat16),
+            pltpu.VMEM((STRAINS * SLICES, PLANE), jnp.bfloat16),
             pltpu.VMEM((STRAINS * SLICES, PLANE), jnp.float32),
             pltpu.VMEM((3 * SLICES, NMOM * PLANE), jnp.bfloat16),
             pltpu.VMEM((SLICES, NMOM * PLANE), jnp.float32),
@@ -481,7 +514,7 @@
         ],
         compiler_params=params(),
         name="solve",
-    )(strain_ids, mine, other, *prepared, forth, back)
+    )(mine, other, *prepared, forth, back)
     fields, projected = pl.pallas_call(
         gather_kernel,
         out_shape=(shape(2, 2, BANDS * PROBES, CELLS), shape(NMOM, 2, PROBES, PROBES)),

time: 56.3 us -> 55.2 us (0.980)
  Pallas kernels: 7.46 us -> 6.03 us
    pallas_call x2, Pallas kernels: 5.65 us -> 4.22 us  [the longest x1 2.54 us: on_device(): pl.pallas_call(prepare, out_shape=(shape(ROWS, STRAINS * SLICES, PTS * CE...]
  transfers between devices with their start and end apart: 1 -> 1, of which waited for: 0 -> 1; matrix products, arithmetic and copies ran while one was open for 0% -> 0% of each run, Pallas kernels for 5% -> 5%
where the time goes in v4:
time: 55.2 us; the launch traced here: 54.9 us
  blocking collectives  47.7 us (86%)
  Pallas kernels  6.03 us (11%)
  between operations  0.68 us (1%)
    all_to_all x2, blocking collectives, exchange(): wide = lax.all_to_all(wide, ALL, split_axis=0, concat_axis=0, tiled=True)  47.7 us
    pallas_call x1, Pallas kernels, on_device(): pl.pallas_call(prepare, out_shape=(shape(ROWS, STRAINS * SLICES, PTS * CE...  2.54 us
    pallas_call x1, Pallas kernels, on_device(): pl.pallas_call(main, out_shape=shape(DEVICES * BACK, CELLS), in_specs=[vm...  1.68 us
  transfers between devices with their start and end apart: 1, of which 1 were waited for; matrix products, arithmetic and copies ran while one was open for 0% of the time, Pallas kernels for 5%

profile of v4, /device:TPU:1, one launch (start us, length us, event | category | flops | bytes accessed | tf_op | source)
XLA Modules:
  0.0 54.9 jit_solution(7615264058586264323)
XLA Ops:
  0.6 1.1 %pack.1 = f32[2560,128]{1,0:T(8,128)S(1)} custom-call(f32[128,128]{1,0:T(8,128)} %bitcast.21, f32[128,128]{1,0:T(8,128)} %bitcast.22, f32[6,4,32]{2,1,0:T(4,128)} %bitcast.23, f32[8,128]{1,0:T(8,128)} %bitcast.24), custom_call_target="tpu_custom_call" | custom-call | tf_op jit(solution)/shard_map/pack/pallas_call | solution.py:441
  1.7 0.0 copy-start
  1.7 0.0 copy-start.1
  1.7 0.0 copy-start.2
  1.7 33.7 %all_to_all.10 = f32[128,5,4,128]{3,2,1,0:T(4,128)S(1)} all-to-all(f32[128,5,4,128]{3,2,1,0:T(4,128)S(1)} %bitcast.18), channel_id=1, replica_groups=mesh['cuts'=32,'tile'=4] {'cuts','tile'}, dimensions={0} | all-to-all | bytes 2621440 | tf_op jit(solution)/shard_map/all_to_all | solution.py:431
  35.5 0.0 copy-start.3
  35.5 0.0 copy-start.4
  35.5 0.4 collective-permute-start
  35.9 0.0 copy-done
  35.9 0.0 copy-done.1
  35.9 0.0 copy-done.2
  35.9 2.5 %prepare.1 = (f32[4,192,1024]{2,1,0:T(8,128)S(1)}, f32[4,32,1024]{2,1,0:T(8,128)S(1)}, f32[32,512]{1,0:T(8,128)S(1)}, f32[32,128]{1,0:T(8,128)S(1)}, bf16[512,512]{1,0:T(8,128)(2,1)S(1)}) custom-call(f32[8]{0:T(128)} %refs_0_.1, f32[2,8,8]{2,1,0:T(8,128)} %refs_1_.1, f32[6,8,8]{2,1,0:T(8,128)} %refs_2_.1, s32[16]{0:T(128)} %refs_3_.1, ...), custom_call_target="tpu_custom_call" | custom-call | tf_op jit(solution)/shard_map/prepare/pallas_call | solution.py:470
  38.4 0.1 collective-permute-done.refs_1_
  38.5 0.0 copy-done.3
  38.5 0.0 copy-done.4
  38.5 1.7 %solve.1 = f32[384,128]{1,0:T(8,128)S(1)} custom-call(f32[2560,128]{1,0:T(8,128)S(1)} %bitcast.17, f32[2560,128]{1,0:T(8,128)S(1)} %collective-permute-done.refs_1_, f32[4,192,1024]{2,1,0:T(8,128)S(1)} %get-tuple-element.9.refs_2_, f32[4,32,1024]{2,1,0:T(8,128)S(1)} %get-tuple-element.10.refs_3_, f32[32,512]{1,0:T(8,128)S(1)} %get-tuple-element.11.refs_4_, ...), custom_call_target="tpu_custom_call" | custom-call | tf_op jit(solution)/shard_map/solve/pallas_call | solution.py:502
  40.2 13.9 %all_to_all.11 = f32[384,1,128]{2,1,0:T(1,128)S(1)} all-to-all(f32[384,1,128]{2,1,0:T(1,128)S(1)} %bitcast.19), channel_id=1, replica_groups=mesh['cuts'=32,'tile'=4] {'cuts','tile'}, dimensions={0} | all-to-all | bytes 393216 | tf_op jit(solution)/shard_map/all_to_all | solution.py:431
  54.2 0.7 %gather.1 = (f32[2,2,128,128]{3,2,1,0:T(8,128)}, f32[4,2,16,16]{3,2,1,0:T(8,128)}) custom-call(f32[384,128]{1,0:T(8,128)S(1)} %bitcast.20), custom_call_target="tpu_custom_call" | custom-call | tf_op jit(solution)/shard_map/gather/pallas_call | solution.py:518
Async XLA Ops:
  1.7 34.2 %copy-start = (bf16[256,768]{1,0:T(8,128)(2,1)S(1)}, bf16[256,768]{1,0:T(8,128)(2,1)}, u32[]{:S(2)}) copy-start(bf16[256,768]{1,0:T(8,128)(2,1)} %constant.10.clone.refs_5_) | copy-start | bytes 1179652
  1.7 34.1 %copy-start.1 = (f32[32,256]{1,0:T(8,128)S(1)}, f32[32,256]{1,0:T(8,128)}, u32[]{:S(2)}) copy-start(f32[32,256]{1,0:T(8,128)} %constant.11.clone.refs_6_) | copy-start | bytes 98308
  1.7 34.1 %copy-start.2 = (f32[32,128]{1,0:T(8,128)S(1)}, f32[32,128]{1,0:T(8,128)}, u32[]{:S(2)}) copy-start(f32[32,128]{1,0:T(8,128)} %constant.12.clone.refs_7_) | copy-start | bytes 49156
  35.5 3.1 %copy-start.3 = (bf16[32,96]{1,0:T(8,128)(2,1)S(1)}, bf16[32,96]{1,0:T(8,128)(2,1)}, u32[]{:S(2)}) copy-start(bf16[32,96]{1,0:T(8,128)(2,1)} %constant.14.clone.refs_8_) | copy-start | bytes 18436
  35.5 3.1 %copy-start.4 = (bf16[32,96]{1,0:T(8,128)(2,1)S(1)}, bf16[32,96]{1,0:T(8,128)(2,1)}, u32[]{:S(2)}) copy-start(bf16[32,96]{1,0:T(8,128)(2,1)} %constant.13.clone.refs_7_) | copy-start | bytes 18436
  35.5 3.1 %collective-permute-start = (f32[2560,128]{1,0:T(8,128)S(1)}, f32[2560,128]{1,0:T(8,128)S(1)}, u32[]{:S(2)}, u32[]{:S(2)}) collective-permute-start(f32[2560,128]{1,0:T(8,128)S(1)} %bitcast.15), channel_id=1, source_target_pairs={{0,4},{4,0},{8,12},{12,8},{16,20},{20,16},{24,28},{28,24},{32,36},... | collective-permute-start | bytes 3932168 | tf_op jit(solution)/shard_map/ppermute | solution.py:462

commit v5 on v4

--- a/solution.py
+++ b/solution.py
@@ -22,7 +22,9 @@
 TERMS = STRAINS + 4
 PLANE = ROWS * CELLS
 DEVICES = SLICES * ROWS
-CHUNK = 20
+CHUNK = 17
+PART = CELLS // 2
+TEST, SLOTS, EDGE, NEXT = 8, 12, 15, 16
 BACK = 3
 NSUB = ROWS * ROWS
 HIGHEST = lax.Precision.HIGHEST
@@ -51,18 +53,41 @@
     copies = [pltpu.make_async_copy(*pair, done.at[i]) for i, pair in enumerate(pairs)]
     for copy in copies:
         copy.start()
+    lane = lax.broadcasted_iota(jnp.int32, (BANDS, CELLS), 1)
+
+    def beside(first, second, side):
+        here = lane[: first.shape[0]] < PART
+        if side == 0:
+            return jnp.where(here, first, pltpu.roll(second, PART, 1))
+        return jnp.where(here, pltpu.roll(first, PART, 1), second)
+
+    def start(band, side, k):
+        return (band * PROBES + side * BANDS + k) * CHUNK
+
     copies[0].wait()
-    for probe in range(PROBES):
-        column = probes_ref[pl.ds(probe, BANDS, stride=PROBES), :]
-        for band in range(BANDS):
-            at = (band * PROBES + probe) * CHUNK
-            out_ref[at : at + 8, :] = column
+    turned = probes_ref[...].T
+    for k in range(BANDS):
+        first = probes_ref[pl.ds(k, BANDS, stride=PROBES), :]
+        second = probes_ref[pl.ds(k + BANDS, BANDS, stride=PROBES), :]
+        for side in range(2):
+            columns = beside(first, second, side)
+            outer = turned[PART - side : PART - side + 1, :]
+            for band in range(BANDS):
+                at = start(band, side, k)
+                out_ref[at : at + BANDS, :] = columns
+                out_ref[at + NEXT : at + NEXT + 1, :] = outer
     copies[1].wait()
-    for probe in range(PROBES):
-        for band in range(BANDS):
-            at = (band * PROBES + probe) * CHUNK
-            first = band * PROBES + 8 * (probe // 4 % 2)
-            out_ref[at + 12 : at + 20, :] = test_ref[first : first + 8, :]
+    for band in range(BANDS):
+        for side in range(2):
+            columns = beside(
+                test_ref[band * PROBES : band * PROBES + 8, :],
+                test_ref[band * PROBES + 8 : band * PROBES + 16, :],
+                side,
+            )
+            for k in range(BANDS):
+                at = start(band, side, k) + TEST
+                half = k // 4
+                out_ref[at : at + 4, :] = columns[4 * half : 4 * half + 4]
     copies[2].wait()
     copies[3].wait()
     piece = lax.axis_index("cuts") % BANDS
@@ -70,11 +95,11 @@
     strain = jnp.concatenate([strain_ref[:, slot, :] for slot in range(ROWS)], axis=1)
     for half in range(2):
         shared = jnp.concatenate([strain[3 * half : 3 * half + 3], edge], axis=0)
-        for probe in range(PROBES):
-            if probe // 4 % 2 == half:
-                for band in range(BANDS):
-                    at = (band * PROBES + probe) * CHUNK
-                    out_ref[at + 8 : at + 12, :] = shared
+        for k in range(4 * half, 4 * half + 4):
+            for band in range(BANDS):
+                for side in range(2):
+                    at = start(band, side, k) + SLOTS
+                    out_ref[at : at + 4, :] = shared
 
 
 def split(value):
@@ -110,10 +135,12 @@
     wave_ref,
     spread_ref,
     cosine_ref,
+    forth_ref,
     result_ref,
     hops_ref,
+    outer_ref,
     own_ref,
-    shift_ref,
+    energy_ref,
     place_ref,
     hop_ref,
     cross_ref,
@@ -127,8 +154,12 @@
     power_ref,
     value_ref,
     across_ref,
+    line_ref,
+    bound_ref,
 ):
     band = lax.axis_index("cuts") // 4
+    side = lax.axis_index("cuts") // 2 % 2
+    k = lax.axis_index("cuts") % 2 * 4 + lax.axis_index("tile")
     pairs = (
         (hop_hbm, hop_ref),
         (cross_hbm, cross_ref),
@@ -164,6 +195,7 @@
     width = CELLS // ROWS
     slot_cell = lax.broadcasted_iota(jnp.int32, (width, PLANE), 0)
     cell = lax.broadcasted_iota(jnp.int32, (width, PLANE), 1)
+    cell = cell // CELLS * CELLS + side * PART + cell % PART
     diagonal = jnp.where(cell % width == slot_cell, cell // width, -1)
     for slot in range(NSUB):
         match = jnp.where(diagonal == ids_ref[slot], 1.0, 0.0)
@@ -191,12 +223,54 @@
     hop = jnp.full((BANDS, CELLS), 2.0 * hop_ref[0], jnp.float32)
     for b in range(1, BANDS):
         hop = jnp.where(sub == b, 2.0 * hop_ref[b], hop)
-    shift_ref[...] = 2.0 * hop_ref[band] * cosine_ref[...]
-
     lane = lax.broadcasted_iota(jnp.int32, (SLICES, CELLS), 1)
 
+    near = lane[:BANDS] < PART
+    owner = lane[:BANDS] // PROBES == sub
+    outer_hop = jnp.sum(jnp.where(owner, hop, 0.0), axis=0, keepdims=True)
+    shift = 2.0 * hop_ref[band] * cosine_ref[...]
+    edges = []
+    for row in range(ROWS):
+        edge = mine_ref[pl.ds(row * CHUNK + EDGE, BANDS, stride=ROWS * CHUNK), :]
+        turned = pltpu.roll(edge, PART, 1)
+        first = jnp.where(side == 0, edge, turned)
+        second = jnp.where(side == 0, turned, edge)
+        line_ref[...] = jnp.where(near, first, second)
+        edges.append(line_ref[...])
+        energy_ref[row] = line_ref[pl.ds(band, 1), :] - shift
+        beyond = jnp.where(lane[:BANDS] == PART - side, edge, 0.0)
+        beyond = jnp.sum(beyond, axis=1, keepdims=True)
+        beyond = jnp.sum(jnp.where(owner, beyond, 0.0), axis=0, keepdims=True)
+        lanes = slice(row * CELLS, (row + 1) * CELLS)
+        high, low = split(mine_ref[pl.ds(row * CHUNK + NEXT, SLICES, stride=ROWS * CHUNK), :])
+        field_ref[0:32, lanes] = high
+        field_ref[32:64, lanes] = low
+        field_ref[64:96, lanes] = high
+        value = matmul(forth_ref[...], field_ref[0:96, lanes])
+        energy = beyond - outer_hop * cosine_ref[...]
+        eighth = energy * energy
+        eighth = eighth * eighth
+        eighth = eighth * eighth
+        value = value * (1.0 / (1.0 + eighth))
+        for field in range(PTS):
+            at = (row * PTS + field) * SLICES
+            bound_ref[at : at + SLICES, :] = value.astype(jnp.bfloat16)
+            value = value * energy
+    sub_two = lax.broadcasted_iota(jnp.int32, (PROBES, CELLS), 0)
+    lane_two = lax.broadcasted_iota(jnp.int32, (PROBES, CELLS), 1)
+    target = jnp.where(side == 0, PART - 1, 0)
+    hit = ((sub_two == k) & (lane_two == target)) | (
+        (sub_two == k + BANDS) & (lane_two == target + PART)
+    )
+    picks = []
+    for src in range(BANDS):
+        entry = jnp.where(side == 0, cross_ref[0, band, src], cross_ref[0, src, band])
+        picks.append(jnp.where(hit, entry, 0.0))
+    picks = jnp.concatenate(picks, axis=0).astype(jnp.bfloat16)
+    outer_ref[...] = matmul(bound_ref[...], picks)
+
     def fields(row, _):
-        edge = mine_ref[pl.ds(row * CHUNK + 11, BANDS, stride=ROWS * CHUNK), :]
+        edge = edges[row]
         for step in range(HALF):
             for pair in range(SLICES // 2):
                 rows = slice(pair * 16, pair * 16 + 16)
@@ -234,8 +308,8 @@
                 from_left = pltpu.roll(product[224:256, own], 1, 1)
                 at = (2 * step + part) * CELLS
                 hops_ref[row, :, at : at + CELLS] = jnp.where(
-                    lane < CELLS - 1, from_right, 0.0
-                ) + jnp.where(lane > 0, from_left, 0.0)
+                    lane % PART < PART - 1, from_right, 0.0
+                ) + jnp.where(lane % PART > 0, from_left, 0.0)
         return 0
 
     for row in range(ROWS):
@@ -253,8 +327,9 @@
     other_ref,
     result_ref,
     hops_ref,
+    outer_ref,
     own_ref,
-    shift_ref,
+    energy_ref,
     place_ref,
     forth_ref,
     back_ref,
@@ -265,14 +340,14 @@
     source_ref,
     moment_ref,
     final_ref,
+    swap_ref,
 ):
     half = lax.axis_index("cuts") % 2
-    band = lax.axis_index("cuts") // 4
 
     for holder in range(ROWS):
         lanes = slice(holder * CELLS, (holder + 1) * CELLS)
         for comp in range(3):
-            rows = pl.ds(holder * CHUNK + 8 + comp, SLICES, stride=ROWS * CHUNK)
+            rows = pl.ds(holder * CHUNK + SLOTS + comp, SLICES, stride=ROWS * CHUNK)
             a = mine_ref[rows, :]
             b = other_ref[rows, :]
             for at, value in ((comp, jnp.where(half == 0, a, b)), (comp + 3, jnp.where(half == 0, b, a))):
@@ -297,10 +372,14 @@
             source_ref[32:64, lanes] = low
             source_ref[64:96, lanes] = high
         coupled = matmul(forth_ref[...], source_ref[:, 0 : PTS * CELLS])
-        terms = [coupled[:, field * CELLS : (field + 1) * CELLS] for field in range(PTS)]
-
-        edge = mine_ref[pl.ds((band * ROWS + row) * CHUNK + 11, 1), :]
-        energy = edge - shift_ref[...]
+        terms = []
+        for field in range(PTS):
+            at = (row * PTS + field) * SLICES
+            terms.append(
+                coupled[:, field * CELLS : (field + 1) * CELLS] + outer_ref[at : at + SLICES, :]
+            )
+
+        energy = energy_ref[row]
         powers = [None, energy]
         for _ in range(2, PTS):
             powers.append(powers[-1] * energy)
@@ -335,47 +414,68 @@
                 out_ref[pl.ds(row * BACK + order, SLICES, stride=ROWS * BACK), :] = value
 
     zero = jnp.zeros((8, CELLS), jnp.float32)
-    near = [zero] * NMOM
-    far = [zero] * NMOM
+    straight = [zero] * NMOM
+    swapped = [zero] * NMOM
+    for row in range(ROWS):
+        for order in range(NMOM):
+            swap_ref[order * ROWS + row] = pltpu.roll(final_ref[order * ROWS + row], PART, 1)
     for s in range(SLICES):
         for row in range(ROWS):
-            at = (s * ROWS + row) * CHUNK + 12
-            test_near = mine_ref[at : at + 8, :]
-            test_far = other_ref[at : at + 8, :]
+            at = (s * ROWS + row) * CHUNK + TEST
+            test = jnp.concatenate([mine_ref[at : at + 4, :], other_ref[at : at + 4, :]], axis=0)
             for order in range(NMOM):
-                value = final_ref[order * ROWS + row, s : s + 1, :]
-                near[order] = near[order] + test_near * value
-                far[order] = far[order] + test_far * value
+                line = order * ROWS + row
+                straight[order] = straight[order] + test * final_ref[line, s : s + 1, :]
+                swapped[order] = swapped[order] + test * swap_ref[line, s : s + 1, :]
     stack = []
     for order in range(NMOM):
-        stack.append(jnp.where(half == 0, near[order], far[order]))
-        stack.append(jnp.where(half == 0, far[order], near[order]))
+        for total in (straight[order], swapped[order]):
+            turned = jnp.concatenate([total[4:8], total[0:4]], axis=0)
+            stack.append(jnp.where(half == 0, total, turned))
+    sub = lax.broadcasted_iota(jnp.int32, (8, CELLS), 0)
+    lane = lax.broadcasted_iota(jnp.int32, (8, CELLS), 1)
     sums = lax.dot_general(
-        jnp.full((8, CELLS), scale, jnp.float32),
+        jnp.where(lane // PART == sub, jnp.float32(scale), 0.0),
         jnp.concatenate(stack, axis=0),
         (((1,), (1,)), ((), ())),
         precision=HIGHEST,
         preferred_element_type=jnp.float32,
     )
-    line = jnp.concatenate([sums, jnp.zeros_like(sums)], axis=1)[0:1]
+    line = jnp.concatenate([sums[0:1], sums[1:2]], axis=1)
     out_ref[pl.ds(2, DEVICES, stride=BACK), :] = jnp.broadcast_to(line, (DEVICES, CELLS))
 
 
 def gather_kernel(blocks_ref, fields_ref, projected_ref):
+    near = lax.broadcasted_iota(jnp.int32, (BANDS, CELLS), 1) < PART
     total = None
     for band in range(BANDS):
-        first = band * PROBES * BACK
-        for order in range(2):
-            fields_ref[order, 0, band * PROBES : (band + 1) * PROBES, :] = blocks_ref[
-                pl.ds(first + order, PROBES, stride=BACK), :
+        for order in range(3):
+            sides = [
+                blocks_ref[
+                    pl.ds((band * PROBES + side * BANDS) * BACK + order, BANDS, stride=BACK), :
+                ]
+                for side in range(2)
             ]
-        part = blocks_ref[pl.ds(first + 2, PROBES, stride=BACK), :]
-        total = part if total is None else total + part
-    turned = total.T
+            if order == 2:
+                part = sides[0] + sides[1]
+                total = part if total is None else total + part
+                continue
+            at = band * PROBES
+            fields_ref[order, 0, at : at + 8, :] = jnp.where(
+                near, sides[0], pltpu.roll(sides[1], PART, 1)
+            )
+            fields_ref[order, 0, at + 8 : at + 16, :] = jnp.where(
+                near, pltpu.roll(sides[0], PART, 1), sides[1]
+            )
     for order in range(2):
         fields_ref[order, 1] = jnp.zeros((BANDS * PROBES, CELLS), jnp.float32)
+    turned = total.T
     for order in range(NMOM):
-        projected_ref[order, 0] = turned[order * PROBES : (order + 1) * PROBES, :]
+        at = order * PROBES
+        projected_ref[order, 0, 0:8, 0:8] = turned[at : at + 8, :]
+        projected_ref[order, 0, 0:8, 8:16] = turned[at + 8 : at + 16, :]
+        projected_ref[order, 0, 8:16, 0:8] = turned[PART + at + 8 : PART + at + 16, :]
+        projected_ref[order, 0, 8:16, 8:16] = turned[PART + at : PART + at + 8, :]
         projected_ref[order, 1] = jnp.zeros((PROBES, PROBES), jnp.float32)
 
 
@@ -424,10 +524,8 @@
     return pltpu.CompilerParams(vmem_limit_bytes=VMEM_BYTES)
 
 
-def exchange(blocks, rows, group):
-    wide = blocks.reshape(DEVICES * rows // group, group, CELLS)
-    if group > 1:
-        wide = wide.reshape(DEVICES, rows // group, group, CELLS)
+def exchange(blocks, rows):
+    wide = blocks.reshape(DEVICES * rows, 1, CELLS)
     wide = lax.all_to_all(wide, ALL, split_axis=0, concat_axis=0, tiled=True)
     return wide.reshape(DEVICES * rows, CELLS)
 
@@ -458,7 +556,7 @@
         far(jnp.transpose(strain_elastic[0], (1, 0, 2))),
         far(band_edge.reshape(BANDS, CELLS)),
     )
-    mine = exchange(outgoing, CHUNK, 4)
+    mine = exchange(outgoing, CHUNK)
     other = lax.ppermute(mine, "cuts", [(i, i ^ 1) for i in range(cut_count)])
     scale = (cut_count * BANDS * ROWS * CELLS) ** (-0.5)
     cosines, wave, spread, cosine, forth, back = constants()
@@ -472,12 +570,13 @@
         out_shape=(
             shape(ROWS, STRAINS * SLICES, PTS * CELLS),
             shape(ROWS, SLICES, PTS * CELLS),
+            shape(ROWS * PTS * SLICES, CELLS),
             shape(SLICES, PLANE),
-            shape(SLICES, CELLS),
+            shape(ROWS, SLICES, CELLS),
             jax.ShapeDtypeStruct((PLANE, PLANE), jnp.bfloat16),
         ),
-        in_specs=[raw] * 4 + [vmem()] * 4,
-        out_specs=(vmem(),) * 5,
+        in_specs=[raw] * 4 + [vmem()] * 5,
+        out_specs=(vmem(),) * 6,
         scratch_shapes=[
             pltpu.SMEM(slice_hop.shape, jnp.float32),
             pltpu.SMEM(cross_hop.shape, jnp.float32),
@@ -491,10 +590,12 @@
             pltpu.VMEM((wide, CELLS), jnp.float32),
             pltpu.VMEM((wide, CELLS), jnp.float32),
             pltpu.VMEM((ROWS, 2 * SLICES, PTS * CELLS), jnp.float32),
+            pltpu.VMEM((BANDS, CELLS), jnp.float32),
+            pltpu.VMEM((ROWS * PTS * SLICES, CELLS), jnp.bfloat16),
         ],
         compiler_params=params(),
         name="prepare",
-    )(*map(far, (slice_hop, cross_hop, deform, strain_ids)), mine, wave, spread, cosine)
+    )(*map(far, (slice_hop, cross_hop, deform, strain_ids)), mine, wave, spread, cosine, forth)
 
     def main(*refs):
         main_kernel(scale, *refs)
@@ -502,7 +603,7 @@
     blocks = pl.pallas_call(
         main,
         out_shape=shape(DEVICES * BACK, CELLS),
-        in_specs=[vmem()] * 9,
+        in_specs=[vmem()] * 10,
         out_specs=vmem(),
         scratch_shapes=[
             pltpu.VMEM((STRAINS * SLICES, PLANE), jnp.bfloat16),
@@ -510,6 +611,7 @@
             pltpu.VMEM((STRAINS * SLICES, PLANE), jnp.float32),
             pltpu.VMEM((3 * SLICES, NMOM * PLANE), jnp.bfloat16),
             pltpu.VMEM((SLICES, NMOM * PLANE), jnp.float32),
+            pltpu.VMEM((NMOM * ROWS, SLICES, CELLS), jnp.float32),
             pltpu.VMEM((NMOM * ROWS, SLICES, CELLS), jnp.float32),
         ],
         compiler_params=params(),
@@ -522,7 +624,7 @@
         out_specs=(vmem(), vmem()),
         compiler_params=params(),
         name="gather",
-    )(exchange(blocks, BACK, 1))
+    )(exchange(blocks, BACK))
     return fields.reshape(2, 2, 1, BANDS, PROBES, 1, CELLS), projected
 
 

time: 55.2 us -> 53.5 us (0.969)
  blocking collectives: 47.7 us -> 45.4 us
  Pallas kernels: 6.03 us -> 6.63 us
    all_to_all x2, blocking collectives: 47.7 us -> 45.4 us  [exchange(): wide = lax.all_to_all(wide, ALL, split_axis=0, concat_axis=0, tiled=True)]
  transfers between devices with their start and end apart: 1 -> 1, of which waited for: 1 -> 0; matrix products, arithmetic and copies ran while one was open for 0% -> 0% of each run, Pallas kernels for 5% -> 5%
where the time goes in v5:
time: 53.5 us; the launch traced here: 53.2 us
  blocking collectives  45.4 us (85%)
  Pallas kernels  6.63 us (12%)
  between operations  0.7 us (1%)
    all_to_all x2, blocking collectives, exchange(): wide = lax.all_to_all(wide, ALL, split_axis=0, concat_axis=0, tiled=True)  45.4 us
    pallas_call x1, Pallas kernels, on_device(): pl.pallas_call(prepare, out_shape=(shape(ROWS, STRAINS * SLICES, PTS * CE...  2.83 us
    pallas_call x1, Pallas kernels, on_device(): pl.pallas_call(main, out_shape=shape(DEVICES * BACK, CELLS), in_specs=[vm...  1.73 us
    pallas_call x1, Pallas kernels, on_device(): pl.pallas_call(pack_kernel, out_shape=shape(DEVICES * CHUNK, CELLS), in_s...  1.21 us
  transfers between devices with their start and end apart: 1, of which 0 were waited for; matrix products, arithmetic and copies ran while one was open for 0% of the time, Pallas kernels for 5%

profile of v5, /device:TPU:1, one launch (start us, length us, event | category | flops | bytes accessed | tf_op | source)
XLA Modules:
  0.0 53.2 jit_solution(2326193881428985178)
XLA Ops:
  0.6 1.2 %pack.1 = f32[2176,128]{1,0:T(8,128)S(1)} custom-call(f32[128,128]{1,0:T(8,128)} %bitcast.23, f32[128,128]{1,0:T(8,128)} %bitcast.24, f32[6,4,32]{2,1,0:T(4,128)} %bitcast.25, f32[8,128]{1,0:T(8,128)} %bitcast.26), custom_call_target="tpu_custom_call" | custom-call | tf_op jit(solution)/shard_map/pack/pallas_call | solution.py:539
  1.9 0.0 copy-start
  1.9 0.0 copy-start.1
  1.9 0.0 copy-start.2
  1.9 0.0 copy-start.3
  1.9 31.6 %all_to_all.10 = f32[2176,1,128]{2,1,0:T(1,128)S(1)} all-to-all(f32[2176,1,128]{2,1,0:T(1,128)S(1)} %bitcast.20), channel_id=1, replica_groups=mesh['cuts'=32,'tile'=4] {'cuts','tile'}, dimensions={0} | all-to-all | bytes 2228224 | tf_op jit(solution)/shard_map/all_to_all | solution.py:529
  33.5 0.0 copy-start.4
  33.5 0.4 collective-permute-start
  33.9 0.0 copy-done
  33.9 0.0 copy-done.1
  33.9 0.0 copy-done.2
  33.9 0.0 copy-done.3
  33.9 2.8 %prepare.1 = (f32[4,192,1024]{2,1,0:T(8,128)S(1)}, f32[4,32,1024]{2,1,0:T(8,128)S(1)}, f32[1024,128]{1,0:T(8,128)S(1)}, f32[32,512]{1,0:T(8,128)S(1)}, f32[4,32,...) custom-call(f32[8]{0:T(128)} %refs_0_.1, f32[2,8,8]{2,1,0:T(8,128)} %refs_1_.1, f32[6,8,8]{2,1,0:T(8,128)} %refs_2_.1, ...), custom_call_target="tpu_custom_call" | custom-call | tf_op jit(solution)/shard_map/prepare/pallas_call | solution.py:568
  36.8 0.0 collective-permute-done.refs_1_
  36.8 0.0 copy-done.4
  36.8 1.7 %solve.1 = f32[384,128]{1,0:T(8,128)S(1)} custom-call(f32[2176,128]{1,0:T(8,128)S(1)} %bitcast.19, f32[2176,128]{1,0:T(8,128)S(1)} %collective-permute-done.refs_1_, f32[4,192,1024]{2,1,0:T(8,128)S(1)} %get-tuple-element.10.refs_2_, f32[4,32,1024]{2,1,0:T(8,128)S(1)} %get-tuple-element.11.refs_3_, f32[1024,128]{1,0:T(8,128)S(1)} %get-tuple-element.12.refs_4_, ...), custom_call_target="tpu_custom_call" | custom-call | tf_op jit(solution)/shard_map/solve/pallas_call | solution.py:603
  38.5 13.8 %all_to_all.11 = f32[384,1,128]{2,1,0:T(1,128)S(1)} all-to-all(f32[384,1,128]{2,1,0:T(1,128)S(1)} %bitcast.22), channel_id=1, replica_groups=mesh['cuts'=32,'tile'=4] {'cuts','tile'}, dimensions={0} | all-to-all | bytes 393216 | tf_op jit(solution)/shard_map/all_to_all | solution.py:529
  52.4 0.9 %gather.1 = (f32[2,2,128,128]{3,2,1,0:T(8,128)}, f32[4,2,16,16]{3,2,1,0:T(8,128)}) custom-call(f32[384,128]{1,0:T(8,128)S(1)} %bitcast.21), custom_call_target="tpu_custom_call" | custom-call | tf_op jit(solution)/shard_map/gather/pallas_call | solution.py:620
Async XLA Ops:
  1.9 32.1 %copy-start = (bf16[256,768]{1,0:T(8,128)(2,1)S(1)}, bf16[256,768]{1,0:T(8,128)(2,1)}, u32[]{:S(2)}) copy-start(bf16[256,768]{1,0:T(8,128)(2,1)} %constant.10.clone.refs_5_) | copy-start | bytes 1179652
  1.9 32.0 %copy-start.1 = (bf16[32,96]{1,0:T(8,128)(2,1)S(1)}, bf16[32,96]{1,0:T(8,128)(2,1)}, u32[]{:S(2)}) copy-start(bf16[32,96]{1,0:T(8,128)(2,1)} %constant.13.clone.refs_8_) | copy-start | bytes 18436
  1.9 32.0 %copy-start.2 = (f32[32,256]{1,0:T(8,128)S(1)}, f32[32,256]{1,0:T(8,128)}, u32[]{:S(2)}) copy-start(f32[32,256]{1,0:T(8,128)} %constant.11.clone.refs_6_) | copy-start | bytes 98308
  1.9 32.0 %copy-start.3 = (f32[32,128]{1,0:T(8,128)S(1)}, f32[32,128]{1,0:T(8,128)}, u32[]{:S(2)}) copy-start(f32[32,128]{1,0:T(8,128)} %constant.12.clone.refs_7_) | copy-start | bytes 49156
  33.5 3.3 %copy-start.4 = (bf16[32,96]{1,0:T(8,128)(2,1)S(1)}, bf16[32,96]{1,0:T(8,128)(2,1)}, u32[]{:S(2)}) copy-start(bf16[32,96]{1,0:T(8,128)(2,1)} %constant.14.clone.refs_9_) | copy-start | bytes 18436
  33.5 3.3 %collective-permute-start = (f32[2176,128]{1,0:T(8,128)S(1)}, f32[2176,128]{1,0:T(8,128)S(1)}, u32[]{:S(2)}, u32[]{:S(2)}) collective-permute-start(f32[2176,128]{1,0:T(8,128)S(1)} %bitcast.17), channel_id=1, source_target_pairs={{0,4},{4,0},{8,12},{12,8},{16,20},{20,16},{24,28},{28,24},{32,36},... | collective-permute-start | bytes 3342344 | tf_op jit(solution)/shard_map/ppermute | solution.py:560

commit v6 on v5

--- a/solution.py
+++ b/solution.py
@@ -22,13 +22,14 @@
 TERMS = STRAINS + 4
 PLANE = ROWS * CELLS
 DEVICES = SLICES * ROWS
-CHUNK = 17
-PART = CELLS // 2
-TEST, SLOTS, EDGE, NEXT = 8, 12, 15, 16
-BACK = 3
+CHUNK = 14
+PARTS = 4
+PART = CELLS // PARTS
+TEST, SLOTS, EDGE = 8, 10, 13
+OUTER, OUTER_EDGE = PART, 3 * PART
+BACK = 4
 NSUB = ROWS * ROWS
 HIGHEST = lax.Precision.HIGHEST
-VMEM_BYTES = 20 * 1024 * 1024
 PASSES = 1
 
 
@@ -55,51 +56,70 @@
         copy.start()
     lane = lax.broadcasted_iota(jnp.int32, (BANDS, CELLS), 1)
 
-    def beside(first, second, side):
-        here = lane[: first.shape[0]] < PART
-        if side == 0:
-            return jnp.where(here, first, pltpu.roll(second, PART, 1))
-        return jnp.where(here, pltpu.roll(first, PART, 1), second)
+    def beside(parts, side):
+        out = None
+        for i, part in enumerate(parts):
+            part = pltpu.roll(part, (i - side) * PART % CELLS, 1)
+            here = lane[: part.shape[0]] // PART == i
+            out = part if out is None else jnp.where(here, part, out)
+        return out
 
     def start(band, side, k):
-        return (band * PROBES + side * BANDS + k) * CHUNK
+        return (band * PROBES + side // 2 * 8 + k * 2 + side % 2) * CHUNK
 
     copies[0].wait()
-    turned = probes_ref[...].T
-    for k in range(BANDS):
-        first = probes_ref[pl.ds(k, BANDS, stride=PROBES), :]
-        second = probes_ref[pl.ds(k + BANDS, BANDS, stride=PROBES), :]
-        for side in range(2):
-            columns = beside(first, second, side)
-            outer = turned[PART - side : PART - side + 1, :]
+    stack = []
+    for k in range(PARTS):
+        parts = [
+            probes_ref[pl.ds(k + PARTS * i, BANDS, stride=PROBES), :] for i in range(PARTS)
+        ]
+        stack += parts
+        for side in range(PARTS):
+            columns = beside(parts, side)
             for band in range(BANDS):
                 at = start(band, side, k)
                 out_ref[at : at + BANDS, :] = columns
-                out_ref[at + NEXT : at + NEXT + 1, :] = outer
+    turned = jnp.concatenate(stack, axis=0).T
+    line = lane[0:1]
+
+    def bordering(k, side):
+        total = jnp.zeros((1, CELLS), jnp.float32)
+        for i, x in enumerate((side * PART - 1, (side + 1) * PART)):
+            if 0 <= x < CELLS:
+                at = OUTER + i * PART
+                row = pltpu.roll(turned[x : x + 1, :], (at - PART * k) % CELLS, 1)
+                total = jnp.where((line >= at) & (line < at + PART), row, total)
+        return total
+
     copies[1].wait()
     for band in range(BANDS):
-        for side in range(2):
-            columns = beside(
-                test_ref[band * PROBES : band * PROBES + 8, :],
-                test_ref[band * PROBES + 8 : band * PROBES + 16, :],
-                side,
-            )
-            for k in range(BANDS):
+        first = band * PROBES
+        parts = [test_ref[first + 4 * i : first + 4 * i + 4, :] for i in range(PARTS)]
+        for side in range(PARTS):
+            columns = beside(parts, side)
+            for k in range(PARTS):
                 at = start(band, side, k) + TEST
-                half = k // 4
-                out_ref[at : at + 4, :] = columns[4 * half : 4 * half + 4]
+                half = k // 2
+                out_ref[at : at + 2, :] = columns[2 * half : 2 * half + 2]
     copies[2].wait()
     copies[3].wait()
     piece = lax.axis_index("cuts") % BANDS
     edge = edge_ref[pl.ds(piece, 1), :]
     strain = jnp.concatenate([strain_ref[:, slot, :] for slot in range(ROWS)], axis=1)
-    for half in range(2):
-        shared = jnp.concatenate([strain[3 * half : 3 * half + 3], edge], axis=0)
-        for k in range(4 * half, 4 * half + 4):
+    for side in range(PARTS):
+        last = pltpu.roll(edge, -side * PART % CELLS, 1)
+        last = jnp.where(line < PART, last, 0.0)
+        for i, x in enumerate((side * PART - 1, (side + 1) * PART)):
+            if 0 <= x < CELLS:
+                beyond = jnp.where(line == x, edge, 0.0)
+                beyond = jnp.sum(beyond, axis=1, keepdims=True)
+                last = jnp.where(line == OUTER_EDGE + i, beyond, last)
+        for k in range(PARTS):
+            half = k // 2
+            shared = jnp.concatenate([strain[3 * half : 3 * half + 3], last + bordering(k, side)])
             for band in range(BANDS):
-                for side in range(2):
-                    at = start(band, side, k) + SLOTS
-                    out_ref[at : at + 4, :] = shared
+                at = start(band, side, k) + SLOTS
+                out_ref[at : at + 4, :] = shared
 
 
 def split(value):
@@ -131,21 +151,22 @@
     cross_hbm,
     deform_hbm,
     ids_hbm,
+    spread_hbm,
+    turns_hbm,
     mine_ref,
     wave_ref,
-    spread_ref,
-    cosine_ref,
-    forth_ref,
     result_ref,
     hops_ref,
     outer_ref,
     own_ref,
     energy_ref,
     place_ref,
+    turns_ref,
     hop_ref,
     cross_ref,
     deform_ref,
     ids_ref,
+    spread_ref,
     done,
     field_ref,
     weights_ref,
@@ -158,13 +179,14 @@
     bound_ref,
 ):
     band = lax.axis_index("cuts") // 4
-    side = lax.axis_index("cuts") // 2 % 2
-    k = lax.axis_index("cuts") % 2 * 4 + lax.axis_index("tile")
+    side = lax.axis_index("cuts") // 2 % 2 * 2 + lax.axis_index("tile") % 2
     pairs = (
         (hop_hbm, hop_ref),
         (cross_hbm, cross_ref),
         (deform_hbm, deform_ref),
         (ids_hbm, ids_ref),
+        (spread_hbm, spread_ref),
+        (turns_hbm, turns_ref),
     )
     copies = [pltpu.make_async_copy(*pair, done.at[i]) for i, pair in enumerate(pairs)]
     for copy in copies:
@@ -214,7 +236,7 @@
                 else:
                     entry = cross_ref[axis, src, band]
             line = jnp.where(source_band == src, entry, line)
-        high, low = split(spread_ref[...] * line)
+        high, low = split(spread_ref[:, 0:256] * line)
         at = slice(term * SLICES, (term + 1) * SLICES)
         for i, part in enumerate((high, high, low)[:PASSES]):
             weights_ref[at, i * 256 : (i + 1) * 256] = part
@@ -225,29 +247,33 @@
         hop = jnp.where(sub == b, 2.0 * hop_ref[b], hop)
     lane = lax.broadcasted_iota(jnp.int32, (SLICES, CELLS), 1)
 
-    near = lane[:BANDS] < PART
-    owner = lane[:BANDS] // PROBES == sub
+    group = lane[:BANDS] // PART
+    owner = (group >= 1) & (group < 3) & (lane[:BANDS] % BANDS == sub)
     outer_hop = jnp.sum(jnp.where(owner, hop, 0.0), axis=0, keepdims=True)
-    shift = 2.0 * hop_ref[band] * cosine_ref[...]
+    cosine = spread_ref[:, 256:384]
+    shift = 2.0 * hop_ref[band] * cosine
     edges = []
     for row in range(ROWS):
         edge = mine_ref[pl.ds(row * CHUNK + EDGE, BANDS, stride=ROWS * CHUNK), :]
-        turned = pltpu.roll(edge, PART, 1)
-        first = jnp.where(side == 0, edge, turned)
-        second = jnp.where(side == 0, turned, edge)
-        line_ref[...] = jnp.where(near, first, second)
-        edges.append(line_ref[...])
+        spread = edge
+        for i in range(1, PARTS):
+            spread = jnp.where(group == i, pltpu.roll(edge, i * PART, 1), spread)
+        line_ref[...] = spread
+        edges.append(spread)
         energy_ref[row] = line_ref[pl.ds(band, 1), :] - shift
-        beyond = jnp.where(lane[:BANDS] == PART - side, edge, 0.0)
-        beyond = jnp.sum(beyond, axis=1, keepdims=True)
+        beyond = [
+            jnp.sum(jnp.where(lane[:BANDS] == OUTER_EDGE + i, edge, 0.0), axis=1, keepdims=True)
+            for i in range(2)
+        ]
+        beyond = jnp.where(group == 1, beyond[0], beyond[1])
         beyond = jnp.sum(jnp.where(owner, beyond, 0.0), axis=0, keepdims=True)
         lanes = slice(row * CELLS, (row + 1) * CELLS)
-        high, low = split(mine_ref[pl.ds(row * CHUNK + NEXT, SLICES, stride=ROWS * CHUNK), :])
+        high, low = split(mine_ref[pl.ds(row * CHUNK + EDGE, SLICES, stride=ROWS * CHUNK), :])
         field_ref[0:32, lanes] = high
         field_ref[32:64, lanes] = low
         field_ref[64:96, lanes] = high
-        value = matmul(forth_ref[...], field_ref[0:96, lanes])
-        energy = beyond - outer_hop * cosine_ref[...]
+        value = matmul(turns_ref[:, 0:96], field_ref[0:96, lanes])
+        energy = beyond - outer_hop * cosine
         eighth = energy * energy
         eighth = eighth * eighth
         eighth = eighth * eighth
@@ -256,17 +282,16 @@
             at = (row * PTS + field) * SLICES
             bound_ref[at : at + SLICES, :] = value.astype(jnp.bfloat16)
             value = value * energy
-    sub_two = lax.broadcasted_iota(jnp.int32, (PROBES, CELLS), 0)
-    lane_two = lax.broadcasted_iota(jnp.int32, (PROBES, CELLS), 1)
-    target = jnp.where(side == 0, PART - 1, 0)
-    hit = ((sub_two == k) & (lane_two == target)) | (
-        (sub_two == k + BANDS) & (lane_two == target + PART)
-    )
-    picks = []
+    sub_two = lax.broadcasted_iota(jnp.int32, (2 * PART, CELLS), 0)
+    lane_two = lax.broadcasted_iota(jnp.int32, (2 * PART, CELLS), 1)
+    entries = jnp.zeros((2 * PART, CELLS), jnp.float32)
     for src in range(BANDS):
-        entry = jnp.where(side == 0, cross_ref[0, band, src], cross_ref[0, src, band])
-        picks.append(jnp.where(hit, entry, 0.0))
-    picks = jnp.concatenate(picks, axis=0).astype(jnp.bfloat16)
+        entry = jnp.where(sub_two < PART, cross_ref[0, src, band], cross_ref[0, band, src])
+        entries = jnp.where(sub_two % BANDS == src, entry, entries)
+    target = sub_two // BANDS % PARTS * PART + jnp.where(sub_two < PART, 0, PART - 1)
+    picks = jnp.where(lane_two == target, entries, 0.0)
+    rest = jnp.zeros((PART, CELLS), jnp.float32)
+    picks = jnp.concatenate([rest, picks, rest], axis=0).astype(jnp.bfloat16)
     outer_ref[...] = matmul(bound_ref[...], picks)
 
     def fields(row, _):
@@ -331,8 +356,7 @@
     own_ref,
     energy_ref,
     place_ref,
-    forth_ref,
-    back_ref,
+    turns_ref,
     out_ref,
     high_ref,
     low_ref,
@@ -340,7 +364,6 @@
     source_ref,
     moment_ref,
     final_ref,
-    swap_ref,
 ):
     half = lax.axis_index("cuts") % 2
 
@@ -371,7 +394,7 @@
             source_ref[0:32, lanes] = high
             source_ref[32:64, lanes] = low
             source_ref[64:96, lanes] = high
-        coupled = matmul(forth_ref[...], source_ref[:, 0 : PTS * CELLS])
+        coupled = matmul(turns_ref[:, 0:96], source_ref[:, 0 : PTS * CELLS])
         terms = []
         for field in range(PTS):
             at = (row * PTS + field) * SLICES
@@ -404,7 +427,7 @@
     source_ref[0:32, :] = high
     source_ref[32:64, :] = low
     source_ref[64:96, :] = high
-    final = matmul(back_ref[...], source_ref[...])
+    final = matmul(turns_ref[:, 96:192], source_ref[...])
     for order in range(NMOM):
         for row in range(ROWS):
             at = order * PLANE + row * CELLS
@@ -413,27 +436,31 @@
             if order < 2:
                 out_ref[pl.ds(row * BACK + order, SLICES, stride=ROWS * BACK), :] = value
 
+    sub = lax.broadcasted_iota(jnp.int32, (8, CELLS), 0)
+    lane = lax.broadcasted_iota(jnp.int32, (8, CELLS), 1)
     zero = jnp.zeros((8, CELLS), jnp.float32)
-    straight = [zero] * NMOM
-    swapped = [zero] * NMOM
-    for row in range(ROWS):
-        for order in range(NMOM):
-            swap_ref[order * ROWS + row] = pltpu.roll(final_ref[order * ROWS + row], PART, 1)
+    totals = [[zero] * PARTS for _ in range(NMOM)]
     for s in range(SLICES):
-        for row in range(ROWS):
-            at = (s * ROWS + row) * CHUNK + TEST
-            test = jnp.concatenate([mine_ref[at : at + 4, :], other_ref[at : at + 4, :]], axis=0)
+        for row in range(0, ROWS, 2):
+            parts = []
+            for i in range(2):
+                at = (s * ROWS + row + i) * CHUNK + TEST
+                parts += [mine_ref[at : at + 2, :], other_ref[at : at + 2, :]]
+            test = jnp.concatenate(parts, axis=0)
+            tests = [test] + [pltpu.roll(test, i * PART, 1) for i in range(1, PARTS)]
             for order in range(NMOM):
                 line = order * ROWS + row
-                straight[order] = straight[order] + test * final_ref[line, s : s + 1, :]
-                swapped[order] = swapped[order] + test * swap_ref[line, s : s + 1, :]
+                value = jnp.where(
+                    sub < 4, final_ref[line, s : s + 1, :], final_ref[line + 1, s : s + 1, :]
+                )
+                for i in range(PARTS):
+                    totals[order][i] = totals[order][i] + tests[i] * value
     stack = []
     for order in range(NMOM):
-        for total in (straight[order], swapped[order]):
-            turned = jnp.concatenate([total[4:8], total[0:4]], axis=0)
+        for i in range(PARTS):
+            total = totals[order][i][0:4] + totals[order][i][4:8]
+            turned = jnp.concatenate([total[2:4], total[0:2]], axis=0)
             stack.append(jnp.where(half == 0, total, turned))
-    sub = lax.broadcasted_iota(jnp.int32, (8, CELLS), 0)
-    lane = lax.broadcasted_iota(jnp.int32, (8, CELLS), 1)
     sums = lax.dot_general(
         jnp.where(lane // PART == sub, jnp.float32(scale), 0.0),
         jnp.concatenate(stack, axis=0),
@@ -441,41 +468,54 @@
         precision=HIGHEST,
         preferred_element_type=jnp.float32,
     )
-    line = jnp.concatenate([sums[0:1], sums[1:2]], axis=1)
-    out_ref[pl.ds(2, DEVICES, stride=BACK), :] = jnp.broadcast_to(line, (DEVICES, CELLS))
+    for i in range(2):
+        line = jnp.concatenate([sums[2 * i : 2 * i + 1], sums[2 * i + 1 : 2 * i + 2]], axis=1)
+        out_ref[pl.ds(2 + i, DEVICES, stride=BACK), :] = jnp.broadcast_to(line, (DEVICES, CELLS))
 
 
 def gather_kernel(blocks_ref, fields_ref, projected_ref):
-    near = lax.broadcasted_iota(jnp.int32, (BANDS, CELLS), 1) < PART
-    total = None
+    group = lax.broadcasted_iota(jnp.int32, (PROBES, CELLS), 1) // PART
+    sums = [None, None]
     for band in range(BANDS):
-        for order in range(3):
+        for order in range(4):
             sides = [
                 blocks_ref[
-                    pl.ds((band * PROBES + side * BANDS) * BACK + order, BANDS, stride=BACK), :
+                    pl.ds(
+                        (band * PROBES + side // 2 * 8 + side % 2) * BACK + order,
+                        PARTS,
+                        stride=2 * BACK,
+                    ),
+                    :,
                 ]
-                for side in range(2)
+                for side in range(PARTS)
             ]
-            if order == 2:
-                part = sides[0] + sides[1]
-                total = part if total is None else total + part
+            if order >= 2:
+                part = (sides[0] + sides[1]) + (sides[2] + sides[3])
+                before = sums[order - 2]
+                sums[order - 2] = part if before is None else before + part
                 continue
-            at = band * PROBES
-            fields_ref[order, 0, at : at + 8, :] = jnp.where(
-                near, sides[0], pltpu.roll(sides[1], PART, 1)
-            )
-            fields_ref[order, 0, at + 8 : at + 16, :] = jnp.where(
-                near, pltpu.roll(sides[0], PART, 1), sides[1]
-            )
+            for i in range(PARTS):
+                total = None
+                for side in range(PARTS):
+                    part = pltpu.roll(sides[side], (side - i) * PART % CELLS, 1)
+                    total = part if total is None else jnp.where(group[:4] == side, part, total)
+                at = band * PROBES + PARTS * i
+                fields_ref[order, 0, at : at + PARTS, :] = total
     for order in range(2):
         fields_ref[order, 1] = jnp.zeros((BANDS * PROBES, CELLS), jnp.float32)
-    turned = total.T
+    turned = jnp.concatenate([sums[0], sums[1]], axis=0).T
     for order in range(NMOM):
-        at = order * PROBES
-        projected_ref[order, 0, 0:8, 0:8] = turned[at : at + 8, :]
-        projected_ref[order, 0, 0:8, 8:16] = turned[at + 8 : at + 16, :]
-        projected_ref[order, 0, 8:16, 0:8] = turned[PART + at + 8 : PART + at + 16, :]
-        projected_ref[order, 0, 8:16, 8:16] = turned[PART + at : PART + at + 8, :]
+        for probe in range(PARTS):
+            first = probe % 2 * 64 + order * 16
+            columns = slice(probe // 2 * PARTS, probe // 2 * PARTS + PARTS)
+            for rotation in range(PARTS):
+                test = (probe - rotation) % PARTS
+                projected_ref[
+                    order,
+                    0,
+                    PARTS * test : PARTS * test + PARTS,
+                    PARTS * probe : PARTS * probe + PARTS,
+                ] = turned[first + 4 * rotation : first + 4 * rotation + 4, columns]
         projected_ref[order, 1] = jnp.zeros((PROBES, PROBES), jnp.float32)
 
 
@@ -505,10 +545,11 @@
     return (
         [float(c) for c in cosine],
         split_constant(np.kron(wave, np.eye(BANDS))),
-        jnp.asarray(spread, jnp.float32),
-        jnp.asarray(np.repeat(cosine[:, None], CELLS, axis=1), jnp.float32),
-        split_constant(wave),
-        split_constant(wave.T),
+        jnp.asarray(
+            np.concatenate([spread, np.repeat(cosine[:, None], CELLS, axis=1)], axis=1),
+            jnp.float32,
+        ),
+        jnp.concatenate([split_constant(wave), split_constant(wave.T)], axis=1),
     )
 
 
@@ -520,8 +561,8 @@
     return jax.ShapeDtypeStruct(dims, jnp.float32)
 
 
-def params():
-    return pltpu.CompilerParams(vmem_limit_bytes=VMEM_BYTES)
+def params(mebibytes):
+    return pltpu.CompilerParams(vmem_limit_bytes=mebibytes * 1024 * 1024)
 
 
 def exchange(blocks, rows):
@@ -548,7 +589,7 @@
             pltpu.VMEM((BANDS, CELLS), jnp.float32),
             pltpu.SemaphoreType.DMA((4,)),
         ],
-        compiler_params=params(),
+        compiler_params=params(8),
         name="pack",
     )(
         far(probes.reshape(BANDS * PROBES, CELLS)),
@@ -559,7 +600,7 @@
     mine = exchange(outgoing, CHUNK)
     other = lax.ppermute(mine, "cuts", [(i, i ^ 1) for i in range(cut_count)])
     scale = (cut_count * BANDS * ROWS * CELLS) ** (-0.5)
-    cosines, wave, spread, cosine, forth, back = constants()
+    cosines, wave, spread, turns = constants()
     wide = SLICES * BANDS
 
     def prepare(*refs):
@@ -574,15 +615,17 @@
             shape(SLICES, PLANE),
             shape(ROWS, SLICES, CELLS),
             jax.ShapeDtypeStruct((PLANE, PLANE), jnp.bfloat16),
+            jax.ShapeDtypeStruct(turns.shape, turns.dtype),
         ),
-        in_specs=[raw] * 4 + [vmem()] * 5,
-        out_specs=(vmem(),) * 6,
+        in_specs=[raw] * 6 + [vmem()] * 2,
+        out_specs=(vmem(),) * 7,
         scratch_shapes=[
             pltpu.SMEM(slice_hop.shape, jnp.float32),
             pltpu.SMEM(cross_hop.shape, jnp.float32),
             pltpu.SMEM(deform.shape, jnp.float32),
             pltpu.SMEM(strain_ids.shape, jnp.int32),
-            pltpu.SemaphoreType.DMA((4,)),
+            pltpu.VMEM(spread.shape, jnp.float32),
+            pltpu.SemaphoreType.DMA((6,)),
             pltpu.VMEM((3 * wide, PLANE), jnp.bfloat16),
             pltpu.VMEM((TERMS * SLICES, PASSES * wide), jnp.bfloat16),
             pltpu.VMEM((ROWS, wide, CELLS), jnp.float32),
@@ -593,9 +636,11 @@
             pltpu.VMEM((BANDS, CELLS), jnp.float32),
             pltpu.VMEM((ROWS * PTS * SLICES, CELLS), jnp.bfloat16),
         ],
-        compiler_params=params(),
+        compiler_params=params(20),
         name="prepare",
-    )(*map(far, (slice_hop, cross_hop, deform, strain_ids)), mine, wave, spread, cosine, forth)
+    )(
+        *map(far, (slice_hop, cross_hop, deform, strain_ids, spread, turns)), mine, wave
+    )
 
     def main(*refs):
         main_kernel(scale, *refs)
@@ -603,7 +648,7 @@
     blocks = pl.pallas_call(
         main,
         out_shape=shape(DEVICES * BACK, CELLS),
-        in_specs=[vmem()] * 10,
+        in_specs=[vmem()] * 9,
         out_specs=vmem(),
         scratch_shapes=[
             pltpu.VMEM((STRAINS * SLICES, PLANE), jnp.bfloat16),
@@ -612,17 +657,16 @@
             pltpu.VMEM((3 * SLICES, NMOM * PLANE), jnp.bfloat16),
             pltpu.VMEM((SLICES, NMOM * PLANE), jnp.float32),
             pltpu.VMEM((NMOM * ROWS, SLICES, CELLS), jnp.float32),
-            pltpu.VMEM((NMOM * ROWS, SLICES, CELLS), jnp.float32),
         ],
-        compiler_params=params(),
+        compiler_params=params(20),
         name="solve",
-    )(mine, other, *prepared, forth, back)
+    )(mine, other, *prepared)
     fields, projected = pl.pallas_call(
         gather_kernel,
         out_shape=(shape(2, 2, BANDS * PROBES, CELLS), shape(NMOM, 2, PROBES, PROBES)),
         in_specs=[vmem()],
         out_specs=(vmem(), vmem()),
-        compiler_params=params(),
+        compiler_params=params(8),
         name="gather",
     )(exchange(blocks, BACK))
     return fields.reshape(2, 2, 1, BANDS, PROBES, 1, CELLS), projected

time: 53.5 us -> 52.5 us (0.981)
  blocking collectives: 45.4 us -> 44.1 us
    all_to_all x2, blocking collectives: 45.4 us -> 44.1 us  [exchange(): wide = lax.all_to_all(wide, ALL, split_axis=0, concat_axis=0, tiled=True)]
where the time goes in v6:
time: 52.5 us; the launch traced here: 52.3 us
  blocking collectives  44.1 us (84%)
  Pallas kernels  7.1 us (14%)
  between operations  0.67 us (1%)
    all_to_all x2, blocking collectives, exchange(): wide = lax.all_to_all(wide, ALL, split_axis=0, concat_axis=0, tiled=True)  44.1 us
    pallas_call x1, Pallas kernels, on_device(): pl.pallas_call(prepare, out_shape=(shape(ROWS, STRAINS * SLICES, PTS * CE...  2.84 us
    pallas_call x1, Pallas kernels, on_device(): pl.pallas_call(main, out_shape=shape(DEVICES * BACK, CELLS), in_specs=[vm...  1.77 us
    pallas_call x1, Pallas kernels, on_device(): pl.pallas_call(pack_kernel, out_shape=shape(DEVICES * CHUNK, CELLS), in_s...  1.43 us
    pallas_call x1, Pallas kernels, on_device(): pl.pallas_call(gather_kernel, out_shape=(shape(2, 2, BANDS * PROBES, CELL...  1.05 us
  transfers between devices with their start and end apart: 1, of which 0 were waited for; matrix products, arithmetic and copies ran while one was open for 0% of the time, Pallas kernels for 5%

profile of v6, /device:TPU:1, one launch (start us, length us, event | category | flops | bytes accessed | tf_op | source)
XLA Modules:
  0.0 52.3 jit_solution(16267475910350987896)
XLA Ops:
  0.6 0.0 copy-start
  0.6 1.4 %pack.1 = f32[1792,128]{1,0:T(8,128)S(1)} custom-call(f32[128,128]{1,0:T(8,128)} %bitcast.23, f32[128,128]{1,0:T(8,128)} %bitcast.24, f32[6,4,32]{2,1,0:T(4,128)} %bitcast.25, f32[8,128]{1,0:T(8,128)} %bitcast.26), custom_call_target="tpu_custom_call" | custom-call | tf_op jit(solution)/shard_map/pack/pallas_call | solution.py:580
  2.1 29.5 %all_to_all.10 = f32[1792,1,128]{2,1,0:T(1,128)S(1)} all-to-all(f32[1792,1,128]{2,1,0:T(1,128)S(1)} %bitcast.20), channel_id=1, replica_groups=mesh['cuts'=32,'tile'=4] {'cuts','tile'}, dimensions={0} | all-to-all | bytes 1835008 | tf_op jit(solution)/shard_map/all_to_all | solution.py:570
  31.6 0.4 collective-permute-start
  32.0 0.0 copy-done
  32.0 2.8 %prepare.1 = (f32[4,192,1024]{2,1,0:T(8,128)S(1)}, f32[4,32,1024]{2,1,0:T(8,128)S(1)}, f32[1024,128]{1,0:T(8,128)S(1)}, f32[32,512]{1,0:T(8,128)S(1)}, f32[4,32,...) custom-call(f32[8]{0:T(128)} %refs_0_.1, f32[2,8,8]{2,1,0:T(8,128)} %refs_1_.1, ...), custom_call_target="tpu_custom_call" | custom-call | tf_op jit(solution)/shard_map/prepare/pallas_call | solution.py:609
  34.8 0.0 collective-permute-done.refs_1_
  34.8 1.8 %solve.1 = f32[512,128]{1,0:T(8,128)S(1)} custom-call(f32[1792,128]{1,0:T(8,128)S(1)} %bitcast.19, f32[1792,128]{1,0:T(8,128)S(1)} %collective-permute-done.refs_1_, f32[4,192,1024]{2,1,0:T(8,128)S(1)} %get-tuple-element.11.refs_2_, f32[4,32,1024]{2,1,0:T(8,128)S(1)} %get-tuple-element.12.refs_3_, f32[1024,128]{1,0:T(8,128)S(1)} %get-tuple-element.13.refs_4_, ...), custom_call_target="tpu_custom_call" | custom-call | tf_op jit(solution)/shard_map/solve/pallas_call | solution.py:648
  36.6 14.6 %all_to_all.11 = f32[512,1,128]{2,1,0:T(1,128)S(1)} all-to-all(f32[512,1,128]{2,1,0:T(1,128)S(1)} %bitcast.22), channel_id=1, replica_groups=mesh['cuts'=32,'tile'=4] {'cuts','tile'}, dimensions={0} | all-to-all | bytes 524288 | tf_op jit(solution)/shard_map/all_to_all | solution.py:570
  51.2 1.1 %gather.1 = (f32[2,2,128,128]{3,2,1,0:T(8,128)}, f32[4,2,16,16]{3,2,1,0:T(8,128)}) custom-call(f32[512,128]{1,0:T(8,128)S(1)} %bitcast.21), custom_call_target="tpu_custom_call" | custom-call | tf_op jit(solution)/shard_map/gather/pallas_call | solution.py:664
Async XLA Ops:
  0.6 31.3 %copy-start = (bf16[256,768]{1,0:T(8,128)(2,1)S(1)}, bf16[256,768]{1,0:T(8,128)(2,1)}, u32[]{:S(2)}) copy-start(bf16[256,768]{1,0:T(8,128)(2,1)} %constant.8.clone.refs_7_) | copy-start | bytes 1179652
  31.6 3.3 %collective-permute-start = (f32[1792,128]{1,0:T(8,128)S(1)}, f32[1792,128]{1,0:T(8,128)S(1)}, u32[]{:S(2)}, u32[]{:S(2)}) collective-permute-start(f32[1792,128]{1,0:T(8,128)S(1)} %bitcast.17), channel_id=1, source_target_pairs={{0,4},{4,0},{8,12},{12,8},{16,20},{20,16},{24,28},{28,24},{32,36},... | collective-permute-start | bytes 2752520 | tf_op jit(solution)/shard_map/ppermute | solution.py:601

commit v7 on v6

--- a/solution.py
+++ b/solution.py
@@ -204,15 +204,14 @@
             field_ref[at : at + 16, lanes] = high
             field_ref[256 + at : 272 + at, lanes] = low
             field_ref[512 + at : 528 + at, lanes] = high
+    for copy in copies:
+        copy.wait()
     waves = matmul(wave_ref[...], field_ref[...])
     for row in range(ROWS):
         waves_ref[row] = waves[:, row * CELLS : (row + 1) * CELLS]
         own_ref[:, row * CELLS : (row + 1) * CELLS] = waves_ref[
             row, pl.ds(band, SLICES, stride=BANDS), :
         ]
-
-    for copy in copies:
-        copy.wait()
 
     width = CELLS // ROWS
     slot_cell = lax.broadcasted_iota(jnp.int32, (width, PLANE), 0)

time: 52.5 us -> 52.6 us (level)
  transfers between devices with their start and end apart: 1 -> 1, of which waited for: 0 -> 0; matrix products, arithmetic and copies ran while one was open for 0% -> 0% of each run, Pallas kernels for 5% -> 6%
where the time goes in v7:
time: 52.6 us; the launch traced here: 52.3 us
  blocking collectives  44.1 us (84%)
  Pallas kernels  7.15 us (14%)
  between operations  0.67 us (1%)
    all_to_all x2, blocking collectives, exchange(): wide = lax.all_to_all(wide, ALL, split_axis=0, concat_axis=0, tiled=True)  44.1 us
    pallas_call x1, Pallas kernels, on_device(): pl.pallas_call(prepare, out_shape=(shape(ROWS, STRAINS * SLICES, PTS * CE...  2.9 us
    pallas_call x1, Pallas kernels, on_device(): pl.pallas_call(main, out_shape=shape(DEVICES * BACK, CELLS), in_specs=[vm...  1.77 us
    pallas_call x1, Pallas kernels, on_device(): pl.pallas_call(pack_kernel, out_shape=shape(DEVICES * CHUNK, CELLS), in_s...  1.43 us
  transfers between devices with their start and end apart: 1, of which 0 were waited for; matrix products, arithmetic and copies ran while one was open for 0% of the time, Pallas kernels for 6%

profile of v7, /device:TPU:1, one launch (start us, length us, event | category | flops | bytes accessed | tf_op | source)
XLA Modules:
  0.0 52.3 jit_solution(816804613001465014)
XLA Ops:
  0.6 0.0 copy-start
  0.6 1.4 %pack.1 = f32[1792,128]{1,0:T(8,128)S(1)} custom-call(f32[128,128]{1,0:T(8,128)} %bitcast.23, f32[128,128]{1,0:T(8,128)} %bitcast.24, f32[6,4,32]{2,1,0:T(4,128)} %bitcast.25, f32[8,128]{1,0:T(8,128)} %bitcast.26), custom_call_target="tpu_custom_call" | custom-call | tf_op jit(solution)/shard_map/pack/pallas_call | solution.py:579
  2.1 29.5 %all_to_all.10 = f32[1792,1,128]{2,1,0:T(1,128)S(1)} all-to-all(f32[1792,1,128]{2,1,0:T(1,128)S(1)} %bitcast.20), channel_id=1, replica_groups=mesh['cuts'=32,'tile'=4] {'cuts','tile'}, dimensions={0} | all-to-all | bytes 1835008 | tf_op jit(solution)/shard_map/all_to_all | solution.py:569
  31.6 0.4 collective-permute-start
  32.0 0.0 copy-done
  32.0 2.9 %prepare.1 = (f32[4,192,1024]{2,1,0:T(8,128)S(1)}, f32[4,32,1024]{2,1,0:T(8,128)S(1)}, f32[1024,128]{1,0:T(8,128)S(1)}, f32[32,512]{1,0:T(8,128)S(1)}, f32[4,32,...) custom-call(f32[8]{0:T(128)} %refs_0_.1, f32[2,8,8]{2,1,0:T(8,128)} %refs_1_.1, ...), custom_call_target="tpu_custom_call" | custom-call | tf_op jit(solution)/shard_map/prepare/pallas_call | solution.py:608
  34.9 0.0 collective-permute-done.refs_1_
  34.9 1.8 %solve.1 = f32[512,128]{1,0:T(8,128)S(1)} custom-call(f32[1792,128]{1,0:T(8,128)S(1)} %bitcast.19, f32[1792,128]{1,0:T(8,128)S(1)} %collective-permute-done.refs_1_, f32[4,192,1024]{2,1,0:T(8,128)S(1)} %get-tuple-element.11.refs_2_, f32[4,32,1024]{2,1,0:T(8,128)S(1)} %get-tuple-element.12.refs_3_, f32[1024,128]{1,0:T(8,128)S(1)} %get-tuple-element.13.refs_4_, ...), custom_call_target="tpu_custom_call" | custom-call | tf_op jit(solution)/shard_map/solve/pallas_call | solution.py:647
  36.7 14.6 %all_to_all.11 = f32[512,1,128]{2,1,0:T(1,128)S(1)} all-to-all(f32[512,1,128]{2,1,0:T(1,128)S(1)} %bitcast.22), channel_id=1, replica_groups=mesh['cuts'=32,'tile'=4] {'cuts','tile'}, dimensions={0} | all-to-all | bytes 524288 | tf_op jit(solution)/shard_map/all_to_all | solution.py:569
  51.3 1.1 %gather.1 = (f32[2,2,128,128]{3,2,1,0:T(8,128)}, f32[4,2,16,16]{3,2,1,0:T(8,128)}) custom-call(f32[512,128]{1,0:T(8,128)S(1)} %bitcast.21), custom_call_target="tpu_custom_call" | custom-call | tf_op jit(solution)/shard_map/gather/pallas_call | solution.py:663
Async XLA Ops:
  0.6 31.3 %copy-start = (bf16[256,768]{1,0:T(8,128)(2,1)S(1)}, bf16[256,768]{1,0:T(8,128)(2,1)}, u32[]{:S(2)}) copy-start(bf16[256,768]{1,0:T(8,128)(2,1)} %constant.8.clone.refs_7_) | copy-start | bytes 1179652
  31.6 3.3 %collective-permute-start = (f32[1792,128]{1,0:T(8,128)S(1)}, f32[1792,128]{1,0:T(8,128)S(1)}, u32[]{:S(2)}, u32[]{:S(2)}) collective-permute-start(f32[1792,128]{1,0:T(8,128)S(1)} %bitcast.17), channel_id=1, source_target_pairs={{0,4},{4,0},{8,12},{12,8},{16,20},{20,16},{24,28},{28,24},{32,36},... | collective-permute-start | bytes 2752520 | tf_op jit(solution)/shard_map/ppermute | solution.py:600
